TPU v7x, 32 devices: a whole 2x2x4 slice. The times are simulated.
32 devices in a mesh: dp: 4 (over z), fsdp: 8 (over y, x, core).
Axes of the slice: x: 2, y: 2, z: 4, core: 2. Of those that a mesh axis runs over, the one named last changes fastest.
Arguments:
- tokens: bfloat16 [32768, 512], P(('dp', 'fsdp')), may hold values from -6 to 6
- halt_in: float32 [32768], P(('dp', 'fsdp')), may hold values from 0 to 0.7
- depths: int32 [32768], P(('dp', 'fsdp')), may hold values from 1 to 8, as said below
- attn_routes: int32 [32768, 4], P(('dp', 'fsdp')), may hold values from 0 to 23, all different within a row
- ffn_routes: int32 [32768, 2], P(('dp', 'fsdp')), may hold values from 0 to 7, all different within a row; in each aligned block of 1024 rows (0 to 1023, 1024 to 2047, ...) at most 512 rows name the same one
- w_query: bfloat16 [512, 1536], P(('dp', 'fsdp')), may hold values from -0.25 to 0.25
- w_out: bfloat16 [1536, 512], P(None, ('dp', 'fsdp')), may hold values from -12 to 12
- w_kv: bfloat16 [512, 128], P(('dp', 'fsdp')), may hold values from -0.25 to 0.25
- router: bfloat16 [512, 32], P(('dp', 'fsdp')), may hold values from -0.15820312 to 0.15820312
- vectors: bfloat16 [5, 512], P(None, ('dp', 'fsdp')), may hold values from -1 to 2
- w_up: bfloat16 [8, 512, 2048], P('fsdp', None, 'dp'), may hold values from -0.25 to 0.25
- w_down: bfloat16 [8, 2048, 512], P('fsdp', 'dp'), may hold values from -0.25 to 0.25
- cot_out: bfloat16 [32768, 512], P(('dp', 'fsdp')), may hold values from -6 to 6
- cot_halt: float32 [32768], P(('dp', 'fsdp')), may hold values from -6 to 6
Outputs:
- block_out: bfloat16 [32768, 512], P(('dp', 'fsdp'))
- halt_out: float32 [32768], P(('dp', 'fsdp'))
- grad_in: bfloat16 [32768, 512], P(('dp', 'fsdp'))
- grad_query: float32 [512, 1536], P(('dp', 'fsdp'))
- grad_out_proj: float32 [1536, 512], P(None, ('dp', 'fsdp'))
- grad_kv: float32 [512, 128], P(('dp', 'fsdp'))
- grad_router: float32 [512, 32], P(('dp', 'fsdp'))
- grad_vectors: float32 [5, 512], P(None, ('dp', 'fsdp'))
- grad_up: float32 [8, 512, 2048], P('fsdp', None, 'dp')
- grad_down: float32 [8, 2048, 512], P('fsdp', 'dp')
Inputs may be any that keep to these rules, and one draw needn't show every extreme that they name: `depths`: halting depth of each token; the first token of every sequence has depth 8. `attn_routes`: each token names 4 different attention experts. `ffn_routes`: each token names 2 different feed-forward experts; among the 1024 rows of one device no expert is named more than 512 times, and in some devices' rows an expert is named exactly 512 times.
All inputs are finite; a program needn't handle non-finite values.
Results may differ from a plain program's by a relative error of at most 0.019.
Values may be sent and summed in bfloat16 or wider, within the bound.
No kernel may reach another device: no remote copies, remote signals or barrier semaphores. Data moves between devices by JAX's collectives and lax.ppermute only.
A program may use at most 256 MiB of HBM per device.

v0:
```python
from functools import partial

import jax
import jax.numpy as jnp
from jax import lax
from jax.experimental import pallas as pl
from jax.experimental.pallas import tpu as pltpu
from jax.sharding import PartitionSpec as P


D = 512
HEAD = 64
A_EXP = 24
A_TOP = 4
F_TOP = 2
STEP = 2
LANES = 128
BLOCK = 256
HALVES = 2
PAIRS = A_EXP // 2
WIDTH = A_EXP * HEAD
KV_AT = 2 * WIDTH
RV_AT = KV_AT + LANES
PACK = RV_AT + LANES
EPSILON = 1e-05
NEG = -1e30
BF = jnp.bfloat16
F32 = jnp.float32

NN = (((1,), (0,)), ((), ()))
NT = (((1,), (1,)), ((), ()))
TN = (((0,), (0,)), ((), ()))

ROOT_MAX = 31.36
ROOT = (
    0.7978849411010742,
    0.03633308410644531,
    -3.259496588725597e-05,
    -5.530620546778664e-05,
    3.964748430007603e-06,
    -1.3226379280695255e-07,
    1.756186418511163e-09,
)
BELL = -0.7213475204444817
BELL_SCALE = 0.3989422804014327


def dot(a, b, dims=NN):
    return lax.dot_general(a, b, dims, preferred_element_type=F32)


def lane_ids(rows):
    return lax.broadcasted_iota(jnp.int32, (rows, LANES), 1)


def norm_stats(values):
    center = values - jnp.mean(values, axis=-1, keepdims=True)
    inv_std = lax.rsqrt(jnp.mean(center * center, axis=-1, keepdims=True) + EPSILON)
    return center * inv_std, inv_std


def norm_back(grad_normed, normal_part, inv_std, gain_row):
    grad_hat = grad_normed * gain_row
    mean_one = jnp.mean(grad_hat, axis=-1, keepdims=True)
    mean_two = jnp.mean(grad_hat * normal_part, axis=-1, keepdims=True)
    return inv_std * (grad_hat - mean_one - normal_part * mean_two)


def transposed_tail(w_ref):
    return turned_tail(w_ref[:, RV_AT:PACK])


def turned_tail(tail):
    eye = (
        lax.broadcasted_iota(jnp.int32, (LANES, LANES), 0)
        == lax.broadcasted_iota(jnp.int32, (LANES, LANES), 1)
    )
    eye = jnp.where(eye, 1.0, 0.0).astype(BF)
    return dot(eye, tail, NT)


def vector_row(rows_t, first, index):
    return rows_t[first + index : first + index + 1, :]


def split_two(values):
    high = values.astype(BF)
    return high, (values - high.astype(F32)).astype(BF)


def ranks_kernel(capacity, meta_ref, pair_ref, rank_ref, rank_t_ref, place_ref, scal_ref):
    tok = meta_ref.shape[0]
    size = capacity // HALVES
    tri = lax.broadcasted_iota(jnp.int32, (BLOCK, BLOCK), 0) >= lax.broadcasted_iota(
        jnp.int32, (BLOCK, BLOCK), 1
    )
    tri = jnp.where(tri, 1.0, 0.0).astype(BF)
    lane = lane_ids(BLOCK)

    def block(b, carry):
        rows = pl.ds(b * BLOCK, BLOCK)
        meta = meta_ref[rows, :]
        pair = pair_ref[rows, :]
        scal_ref[rows, :] = jnp.where(lane == 0, pair[:, 0:1], pair[:, 1:2])
        pick = ((lane == meta[:, 4:5]) | (lane == meta[:, 5:6])) & (meta[:, 6:7] >= STEP)
        ones = jnp.where(pick, 1.0, 0.0)
        count = dot(tri, ones.astype(BF)) + carry
        rank = jnp.where(pick, count - 1.0, -1.0)
        rank_ref[rows, :] = rank
        place = jnp.full((BLOCK, LANES), -1, jnp.int32)
        for k in range(F_TOP):
            route = meta[:, 4 + k : 5 + k]
            mine = jnp.sum(jnp.where(lane == route, rank, 0.0), axis=1, keepdims=True)
            mine = mine.astype(jnp.int32)
            for h in range(HALVES):
                within = mine - h * size
                dest = jnp.where((within >= 0) & (within < size), route * size + within, -1)
                place = jnp.where(lane == F_TOP * h + k, dest, place)
        place_ref[rows, :] = place
        return count[BLOCK - 1 :, :]

    lax.fori_loop(0, tok // BLOCK, block, jnp.zeros((1, LANES), F32))
    rank_t_ref[...] = jnp.transpose(rank_ref[...])[: rank_t_ref.shape[0], :].astype(jnp.int32)


def gather_pair(rank_t_ref, rows_ref, starts, slots_refs, pair):
    hots, targets = [], []
    for e in (2 * pair, 2 * pair + 1):
        row = rank_t_ref[pl.ds(e, 1), :]
        for start, slots_ref in zip(starts, slots_refs):
            size = slots_ref.shape[1]
            place = lax.broadcasted_iota(jnp.int32, (size, row.shape[1]), 0) + start
            hots.append(jnp.where(place == row, 1.0, 0.0).astype(BF))
            targets.append((slots_ref, e, size))
    rows = dot(jnp.concatenate(hots, axis=0), rows_ref[...]).astype(BF)
    at = 0
    for slots_ref, e, size in targets:
        slots_ref[e] = rows[at : at + size]
        at += size


def gather_kernel(experts, starts, rank_t_ref, rows_ref, *slots_refs):
    def gather(pair, _):
        gather_pair(rank_t_ref, rows_ref, starts, slots_refs, pair)
        return 0

    lax.fori_loop(0, experts // 2, gather, 0)


def one_hot(rank_t_ref, e, capacity):
    row = rank_t_ref[pl.ds(e, 1), :]
    place = lax.broadcasted_iota(jnp.int32, (capacity, row.shape[1]), 0)
    return jnp.where(place == row, 1.0, 0.0).astype(BF)


def select_heads(values, route, lane_half):
    shifted = route - lane_half
    acc = jnp.zeros((values.shape[0], LANES), F32)
    for p in range(PAIRS):
        acc = jnp.where(shifted == 2 * p, values[:, p * LANES : (p + 1) * LANES], acc)
    return acc + pltpu.roll(acc, HEAD, 1)


def spread_heads(pairs, meta, lane, lane_half, store):
    doubled, shifted = [], []
    for k in range(A_TOP):
        half = (lane >= HEAD) if k % 2 else (lane < HEAD)
        part = jnp.where(half, pairs[k // 2], 0.0)
        doubled.append(part + pltpu.roll(part, HEAD, 1))
        shifted.append(meta[:, k : k + 1] - lane_half)
    for p in range(PAIRS):
        acc = jnp.zeros(doubled[0].shape, F32)
        for k in range(A_TOP):
            acc = jnp.where(shifted[k] == 2 * p, doubled[k], acc)
        store(p, acc.astype(BF))


def place_pieces(shape, pieces, w_ref):
    groups, experts, shard = shape
    if len(pieces) == 1:
        w_ref[...] = pieces[0][...]
        return
    mine, group = lax.axis_index("fsdp"), lax.axis_index("dp")
    for m in range(experts):
        base = jnp.bitwise_xor(mine, m) * shard
        for g in range(groups):
            owner = lax.rem(group + g, groups)
            if m < 6:
                block = pieces[m][g]
            else:
                low, high = pieces[6 + 2 * (m - 6)], pieces[7 + 2 * (m - 6)]
                block = low[g] if g < groups // 2 else high[g - groups // 2]
            rows = pl.ds(pl.multiple_of(owner * experts * shard + base, shard), shard)
            w_ref[rows, :] = block


def attend_kernel(experts, shape, *refs):
    tok_ref, meta_ref, rank_t_ref = refs[:3]
    pieces, outs, refs = refs[3:-25], refs[-25:-14], refs[-14:]
    w_ref, slotq_ref, kv_ref, so_ref, lse_ref, gates_ref, mixed_ref, hidden_ref, fgate_ref = refs[:9]
    n2_ref, slots_ref, kx_ref, vx_ref, sems = refs[9:]
    place_pieces(shape, pieces, w_ref)
    tok = tok_ref.shape[0]
    whole_copies = {
        i: pltpu.make_async_copy(refs[i], outs[i], sems.at[i, 0]) for i in (0, 1, 2, 3, 4, 5)
    }
    whole_copies[0].start()

    def row_copies(b, rows):
        return [
            pltpu.make_async_copy(refs[i].at[rows], outs[i].at[rows], sems.at[i, b])
            for i in (6, 7, 8, 9)
        ]

    first = A_EXP + experts
    rows_t = transposed_tail(w_ref)
    gain_one, shift_one, gain_two, shift_two = (vector_row(rows_t, first, i) for i in range(4))
    lane = lane_ids(BLOCK)
    upper = lane >= HEAD
    lane_half = jnp.where(upper, 1, 0)

    def project(b, _):
        rows = pl.ds(b * BLOCK, BLOCK)
        meta = meta_ref[rows, :]
        hat, _ = norm_stats(tok_ref[rows, :].astype(F32))
        normed = (hat * gain_one + shift_one).astype(BF)
        queries = dot(normed, w_ref[:, :WIDTH])
        kv = dot(normed, w_ref[:, KV_AT:RV_AT])
        logits = dot(normed, w_ref[:, RV_AT:PACK])
        kv_ref[rows, :] = kv.astype(BF)
        swapped = pltpu.roll(kv, HEAD, 1)
        kx_ref[0, rows, :] = jnp.where(upper, 0.0, kv).astype(BF)
        kx_ref[1, rows, :] = jnp.where(upper, swapped, 0.0).astype(BF)
        vx_ref[0, rows, :] = jnp.where(upper, 0.0, swapped).astype(BF)
        vx_ref[1, rows, :] = jnp.where(upper, kv, 0.0).astype(BF)
        picked = [select_heads(queries, meta[:, k : k + 1], lane_half) for k in range(A_TOP)]
        for j in range(A_TOP // 2):
            slotq_ref[j, rows, :] = jnp.where(upper, picked[2 * j + 1], picked[2 * j]).astype(BF)
        chosen = [
            jnp.sum(jnp.where(lane == meta[:, k : k + 1], logits, 0.0), axis=1, keepdims=True)
            for k in range(A_TOP)
        ]
        top = jnp.maximum(jnp.maximum(chosen[0], chosen[1]), jnp.maximum(chosen[2], chosen[3]))
        raised = [jnp.exp(c - top) for c in chosen]
        scale = 1.0 / (raised[0] + raised[1] + raised[2] + raised[3])
        gates = jnp.zeros((BLOCK, LANES), F32)
        for k in range(A_TOP):
            gates = jnp.where(lane == k, raised[k] * scale, gates)
        gates_ref[rows, :] = gates
        return 0

    lax.fori_loop(0, tok // BLOCK, project, 0)
    for i in (1, 2, 5):
        whole_copies[i].start()

    below = lax.broadcasted_iota(jnp.int32, (BLOCK, BLOCK), 1) <= lax.broadcasted_iota(
        jnp.int32, (BLOCK, BLOCK), 0
    )
    for i in range(tok // BLOCK):
        rows = slice(i * BLOCK, (i + 1) * BLOCK)
        seen = (i + 1) * BLOCK
        lse_ref[rows, :] = jnp.zeros((BLOCK, LANES), F32)

        def pair(j, _, rows=rows, seen=seen, i=i):
            out = jnp.zeros((BLOCK, LANES), F32)
            query = slotq_ref[j, rows, :]
            logs = lse_ref[rows, :]
            for h in range(2):
                scores = dot(query, kx_ref[h, :seen, :], NT) * (HEAD**-0.5)
                last = jnp.where(below, scores[:, i * BLOCK :], NEG)
                scores = last if i == 0 else jnp.concatenate([scores[:, : i * BLOCK], last], axis=1)
                top = jnp.max(scores, axis=1, keepdims=True)
                raised = jnp.exp(scores - top)
                total = jnp.sum(raised, axis=1, keepdims=True)
                probs = (raised * (1.0 / total)).astype(BF)
                out = out + dot(probs, vx_ref[h, :seen, :])
                logs = jnp.where(lane == 2 * j + h, top + jnp.log(total), logs)
            so_ref[j, rows, :] = out
            lse_ref[rows, :] = logs
            return 0

        lax.fori_loop(0, A_TOP // 2, pair, 0)

    for i in (3, 4):
        whole_copies[i].start()

    def finish(b, _):
        rows = pl.ds(b * BLOCK, BLOCK)
        meta = meta_ref[rows, :]
        gates = gates_ref[rows, :]
        active = jnp.where(meta[:, 6:7] >= STEP, 1.0, 0.0)
        pairs = [
            so_ref[j, rows, :]
            * jnp.where(upper, gates[:, 2 * j + 1 : 2 * j + 2], gates[:, 2 * j : 2 * j + 1])
            for j in range(A_TOP // 2)
        ]

        def store(p, block):
            mixed_ref[rows, p * LANES : (p + 1) * LANES] = block

        spread_heads(pairs, meta, lane, lane_half, store)
        branch = dot(mixed_ref[rows, :], w_ref[:, WIDTH:KV_AT], NT)
        hidden = tok_ref[rows, :].astype(F32) + active * branch
        hidden_ref[rows, :] = hidden
        hat, _ = norm_stats(hidden)
        normed = (hat * gain_two + shift_two).astype(BF)
        n2_ref[rows, :] = normed
        logits = dot(normed, w_ref[:, RV_AT:PACK])
        first_logit, second_logit = (
            jnp.sum(
                jnp.where(lane == meta[:, 4 + k : 5 + k] + A_EXP, logits, 0.0), axis=1, keepdims=True
            )
            for k in range(F_TOP)
        )
        top = jnp.maximum(first_logit, second_logit)
        first_raised, second_raised = jnp.exp(first_logit - top), jnp.exp(second_logit - top)
        scale = 1.0 / (first_raised + second_raised)
        fgate_ref[rows, :] = jnp.where(lane == 0, first_raised * scale, second_raised * scale)
        for copy in row_copies(b, rows):
            copy.start()
        return 0

    lax.fori_loop(0, tok // BLOCK, finish, 0)

    def slots_copy(pair):
        both = pl.ds(2 * pair, 2)
        return pltpu.make_async_copy(slots_ref.at[both], outs[10].at[both], sems.at[10, pair])

    def gather(pair, _):
        gather_pair(rank_t_ref, n2_ref, (0,), (slots_ref,), pair)
        slots_copy(pair).start()
        return 0

    lax.fori_loop(0, experts // 2, gather, 0)
    for pair in range(experts // 2):
        slots_copy(pair).wait()
    for copy in whole_copies.values():
        copy.wait()
    for b in range(tok // BLOCK):
        for copy in row_copies(b, pl.ds(b * BLOCK, BLOCK)):
            copy.wait()


def expert_kernel(parts, x_ref, up_ref, down_ref, out_ref, act_ref, slope_ref, total_ref):
    total_ref[...] = jnp.zeros(total_ref.shape, F32)

    def part(c, _):
        pre = dot(x_ref[...], up_ref[c])
        square = pre * pre
        short = jnp.minimum(square, ROOT_MAX)
        root = ROOT[-1] * short
        for coef in ROOT[-2:0:-1]:
            root = (root + coef) * short
        phi = 0.5 + 0.5 * jnp.tanh(pre * (root + ROOT[0]))
        act = (pre * phi).astype(BF)
        act_ref[c] = act
        bell = jnp.exp2(square * BELL)
        slope_ref[c] = (phi + (pre * BELL_SCALE) * bell).astype(BF)
        total_ref[...] += dot(act, down_ref[c])
        return 0

    lax.fori_loop(0, parts, part, 0, unroll=2)
    out_ref[...] = total_ref[...].astype(BF)


def combine_sums(h, place, back_ref, fgate, cot, halt_row, lane, branch, cols):
    slot = lax.broadcasted_iota(jnp.int32, (BLOCK, back_ref.shape[0]), 1)
    for k in range(F_TOP):
        at = F_TOP * h + k
        hot = jnp.where(slot == place[:, at : at + 1], 1.0, 0.0).astype(BF)
        came = dot(hot, back_ref[...])
        branch = branch + fgate[:, k : k + 1] * came
        one = jnp.sum(came * cot, axis=1, keepdims=True)
        two = jnp.sum(came * halt_row, axis=1, keepdims=True)
        cols = cols + jnp.where(lane == k, one, jnp.where(lane == F_TOP + k, two, 0.0))
    return branch, cols


def split_three(values):
    high = values.astype(BF).astype(F32)
    middle = (values - high).astype(BF).astype(F32)
    return high, middle, values - high - middle


def combine_first_kernel(
    experts,
    back_ref,
    place_ref,
    tail_ref,
    meta_ref,
    fgate_ref,
    cot_ref,
    branch_ref,
    cols_ref,
    live_ref,
    dense_ref,
):
    halt_row = vector_row(turned_tail(tail_ref[...]), A_EXP + experts, 4)
    lane = lane_ids(BLOCK)

    def block(b, _):
        rows = pl.ds(b * BLOCK, BLOCK)
        meta = meta_ref[rows, :]
        fgate = fgate_ref[rows, :]
        branch, cols = combine_sums(
            0,
            place_ref[rows, :],
            back_ref,
            fgate,
            cot_ref[rows, :].astype(F32),
            halt_row,
            lane,
            jnp.zeros((BLOCK, D), F32),
            jnp.zeros((BLOCK, LANES), F32),
        )
        branch_ref[rows, :] = branch
        cols_ref[rows, :] = cols
        active = jnp.where(meta[:, 6:7] >= STEP, 1.0, 0.0)
        dense = jnp.zeros((BLOCK, LANES), F32)
        for k in range(F_TOP):
            named = lane == meta[:, 4 + k : 5 + k]
            dense = jnp.where(named, active * fgate[:, k : k + 1], dense)
        dense_ref[rows, :] = dense
        return 0

    lax.fori_loop(0, branch_ref.shape[0] // BLOCK, block, 0)
    turned = jnp.transpose(dense_ref[...])[: live_ref.shape[1], :]
    for index, part in enumerate(split_three(turned)):
        live_ref[index] = part.astype(BF)


def combine_kernel(
    experts,
    capacity,
    back_ref,
    branch_ref,
    cols_ref,
    live_ref,
    place_ref,
    rank_t_ref,
    hidden_ref,
    tail_ref,
    meta_ref,
    fgate_ref,
    scal_ref,
    cot_ref,
    out_ref,
    halt_ref,
    slope_ref,
    glf_ref,
    row_ref,
    ab_ref,
    kept_ref,
):
    step = pl.program_id(0)
    halt_row = vector_row(turned_tail(tail_ref[...]), A_EXP + experts, 4)
    lane = lane_ids(BLOCK)

    @pl.when(step == 0)
    def _():
        row_ref[...] = jnp.zeros(row_ref.shape, F32)

    meta = meta_ref[...]
    fgate = fgate_ref[...]
    scal = scal_ref[...]
    active = jnp.where(meta[:, 6:7] >= STEP, 1.0, 0.0)
    branch, cols = combine_sums(
        1,
        place_ref[...],
        back_ref,
        fgate,
        cot_ref[...].astype(F32),
        halt_row,
        lane,
        branch_ref[...],
        cols_ref[...],
    )
    z = hidden_ref[...] + active * branch
    out_ref[...] = z.astype(BF)
    prob = 1.0 / (1.0 + jnp.exp(-jnp.sum(z * halt_row, axis=1, keepdims=True)))
    halt_in, cot_halt = scal[:, 0:1], scal[:, 1:2]
    room = active * (1.0 - halt_in) * prob
    slope = cot_halt * room * (1.0 - prob)
    halt_ref[...] = jnp.broadcast_to(halt_in + room, (BLOCK, LANES))
    wide_slope = jnp.broadcast_to(slope, (BLOCK, LANES))
    slope_ref[...] = wide_slope
    kept_ref[pl.ds(step * BLOCK, BLOCK), :] = wide_slope
    row_ref[0:1, :] += jnp.sum(slope * z, axis=0, keepdims=True)
    gfg = [active * (cols[:, k : k + 1] + slope * cols[:, 2 + k : 3 + k]) for k in range(F_TOP)]
    inner = fgate[:, 0:1] * gfg[0] + fgate[:, 1:2] * gfg[1]
    glf = jnp.zeros((BLOCK, LANES), F32)
    for k in range(F_TOP):
        value = fgate[:, k : k + 1] * (gfg[k] - inner)
        glf = jnp.where(lane == meta[:, 4 + k : 5 + k] + A_EXP, value, glf)
    glf_ref[...] = glf

    @pl.when(step == pl.num_programs(0) - 1)
    def _():
        slopes = [part[:1, :] for part in split_three(jnp.transpose(kept_ref[...]))]
        low = [live_ref[i].astype(F32) for i in range(3)]
        tok = kept_ref.shape[0]
        for e in range(experts):
            rows = [part[e : e + 1, :] for part in low] + slopes + [jnp.zeros((2, tok), F32)]
            rows = jnp.concatenate(rows, axis=0).astype(BF)
            ab_ref[e] = dot(rows, one_hot(rank_t_ref, e, capacity), NT).astype(BF)


def data_back_kernel(experts, parts, h, *refs):
    cot_refs, refs = refs[:-8], refs[-8:]
    ab_ref, tail_ref, slope_ref, up_ref, down_ref, gpre_ref, gy_ref, rows_ref = refs
    size = ab_ref.shape[2] // HALVES
    count = ab_ref.shape[0]
    rows = count * size
    halt_row = vector_row(turned_tail(tail_ref[...]), A_EXP + experts, 4)
    cols = []
    cots = []
    for i in range(count):
        ab = ab_ref[i].astype(F32)[:, h * size : (h + 1) * size]
        live = ab[0:1, :] + ab[1:2, :] + ab[2:3, :]
        slope = ab[3:4, :] + ab[4:5, :] + ab[5:6, :]
        filler = jnp.zeros((LANES - 2, size), F32)
        cols.append(jnp.transpose(jnp.concatenate([live, slope, filler], axis=0)))
        for ref in cot_refs:
            part = ref.shape[0] // count
            cots.append(ref[i * part : (i + 1) * part, :].astype(F32))
    cols = jnp.concatenate(cols, axis=0)
    cots = jnp.concatenate(cots, axis=0)
    gy = (cols[:, 0:1] * (cots + cols[:, 1:2] * halt_row)).astype(BF)
    gy_ref[...] = gy
    total = jnp.zeros((rows, D), F32)
    for c in range(parts):
        gpre = (dot(gy, down_ref[c], NT) * slope_ref[c].astype(F32)).astype(BF)
        gpre_ref[c] = gpre
        total = total + dot(gpre, up_ref[c], NT)
    rows_ref[...] = total.astype(BF)


def weight_back_kernel(parts, steps, joined, *refs):
    up_acc, down_acc = refs[-2:]
    step = pl.program_id(0)

    @pl.when(step == 0)
    def _():
        up_acc[...] = jnp.zeros(up_acc.shape, F32)
        down_acc[...] = jnp.zeros(down_acc.shape, F32)

    for h in range(HALVES):
        x_ref, gy_ref, gpre_ref, act_ref = refs[4 * h : 4 * h + 4]

        @pl.when(step // steps == h)
        def _(x_ref=x_ref, gy_ref=gy_ref, gpre_ref=gpre_ref, act_ref=act_ref):
            for c in range(parts):
                up_acc[c] += dot(x_ref[...], gpre_ref[c], TN)
                down_acc[c] += dot(gy_ref[...], act_ref[c], TN)

    @pl.when(step == pl.num_programs(0) - 1)
    def _():
        for c in range(parts):
            if joined:
                refs[-3][c, :D] = up_acc[c].astype(BF)
                refs[-3][c, D:] = jnp.transpose(down_acc[c]).astype(BF)
            else:
                refs[-4][c] = up_acc[c].astype(BF)
                refs[-3][c] = jnp.transpose(down_acc[c]).astype(BF)


def store_grads(ref, values, start):
    columns = slice(start, start + values.shape[1])
    if len(ref.shape) == 2:
        ref[:, columns] = values
        return
    if len(ref.shape) == 5:
        _, chips, groups, shard, _ = ref.shape
        core = jnp.bitwise_and(lax.axis_index("fsdp"), 1)
        for e in range(2 * chips):
            for g in range(groups):
                at = (g * 2 * chips + e) * shard
                side = jnp.bitwise_xor(core, e % 2)
                ref[side, e // 2, g, :, columns] = values[at : at + shard]
        return
    experts, groups, shard, _ = ref.shape
    for e in range(experts):
        for g in range(groups):
            at = (g * experts + e) * shard
            ref[e, g, :, columns] = values[at : at + shard]


def hidden_back_kernel(
    experts,
    capacity,
    first_ref,
    second_ref,
    rank_ref,
    hidden_ref,
    w_ref,
    tail_ref,
    meta_ref,
    cot_ref,
    slope_ref,
    glf_ref,
    mixed_ref,
    so_ref,
    gates_ref,
    lse_ref,
    gout_ref,
    gh_ref,
    gslot_ref,
    gla_ref,
    logs_ref,
    rv_ref,
    vec_ref,
    acc_ref,
):
    step = pl.program_id(0)
    count = hidden_ref.shape[0]
    first = A_EXP + experts
    size = capacity // HALVES
    rows_t = turned_tail(tail_ref[...])
    low_t = rows_t.astype(BF)
    gain_two, shift_two, halt_row = (vector_row(rows_t, first, i) for i in (2, 3, 4))
    lane = lane_ids(count)
    upper = lane >= HEAD
    lane_half = jnp.where(upper, 1, 0)

    @pl.when(step == 0)
    def _():
        vec_ref[...] = jnp.zeros(vec_ref.shape, F32)
        acc_ref[...] = jnp.zeros(acc_ref.shape, F32)
        rv_ref[...] = jnp.zeros(rv_ref.shape, F32)

    meta = meta_ref[...]
    rank = rank_ref[...].astype(jnp.int32)
    active = jnp.where(meta[:, 6:7] >= STEP, 1.0, 0.0)
    place = lax.broadcasted_iota(jnp.int32, (count, size), 1)
    glf_high, glf_low = split_two(glf_ref[...])
    grad = dot(glf_high, low_t) + dot(glf_low, low_t)
    for h, back_ref in enumerate((first_ref, second_ref)):
        for e in range(experts):
            hot = jnp.where(place + h * size == rank[:, e : e + 1], 1.0, 0.0).astype(BF)
            grad = grad + dot(hot, back_ref[e])
    hat, inv = norm_stats(hidden_ref[...])
    normed = (hat * gain_two + shift_two).astype(BF)
    rv_ref[...] += dot(normed, glf_high, TN) + dot(normed, glf_low, TN)
    vec_ref[2:3, :] += jnp.sum(grad * hat, axis=0, keepdims=True)
    vec_ref[3:4, :] += jnp.sum(grad, axis=0, keepdims=True)
    gz = cot_ref[...].astype(F32) + slope_ref[:, 0:1] * halt_row
    gh = gz + norm_back(grad, hat, inv, gain_two)
    gh_ref[...] = gh
    ga = (active * gh).astype(BF)
    acc_ref[...] += dot(ga, mixed_ref[...], TN)
    gm = dot(ga, w_ref[...])
    gates = gates_ref[...]
    weighted = jnp.zeros((count, 1), F32)
    grads = []
    picked = [select_heads(gm, meta[:, k : k + 1], lane_half) for k in range(A_TOP)]
    for j in range(A_TOP // 2):
        both = jnp.where(upper, picked[2 * j + 1], picked[2 * j])
        prod = both * so_ref[j]
        scale = jnp.where(upper, gates[:, 2 * j + 1 : 2 * j + 2], gates[:, 2 * j : 2 * j + 1])
        gslot_ref[j] = (both * scale).astype(BF)
        grads.append(jnp.sum(jnp.where(upper, 0.0, prod), axis=1, keepdims=True))
        grads.append(jnp.sum(jnp.where(upper, prod, 0.0), axis=1, keepdims=True))
    logs = lse_ref[...]
    for k in range(A_TOP):
        inner = gates[:, k : k + 1] * grads[k]
        weighted = weighted + inner
        logs = jnp.where(lane == A_TOP + k, inner, logs)
    logs_ref[...] = logs
    gla = jnp.zeros((count, LANES), F32)
    for k in range(A_TOP):
        value = gates[:, k : k + 1] * (grads[k] - weighted)
        gla = jnp.where(lane == meta[:, k : k + 1], value, gla)
    gla_ref[...] = gla

    @pl.when(step == pl.num_programs(0) - 1)
    def _():
        store_grads(gout_ref, acc_ref[...].astype(BF), 0)


def input_back_kernel(
    experts,
    tok_ref,
    w_ref,
    meta_ref,
    gh_ref,
    gslot_ref,
    gla_ref,
    rvin_ref,
    vecin_ref,
    halt_ref,
    lse_ref,
    slotq_ref,
    kv_ref,
    gin_ref,
    pack_ref,
    gx_ref,
    wide_ref,
    acc_ref,
    rv_ref,
    vec_ref,
    kx_ref,
    vx_ref,
    lset_ref,
    gq_ref,
):
    tok = tok_ref.shape[0]
    blocks = tok // BLOCK
    first = A_EXP + experts
    rows_t = transposed_tail(w_ref)
    low_t = rows_t.astype(BF)
    gain_one, shift_one = (vector_row(rows_t, first, i) for i in range(2))
    lane = lane_ids(BLOCK)
    upper = lane >= HEAD
    lane_half = jnp.where(upper, 1, 0)
    all_upper = lane_ids(tok) >= HEAD
    vec_ref[...] = jnp.zeros(vec_ref.shape, F32)
    vec_ref[2:4, :] = vecin_ref[2:4, :]
    vec_ref[4:5, :] = halt_ref[0:1, :]
    acc_ref[...] = jnp.zeros(acc_ref.shape, F32)
    rv_ref[...] = rvin_ref[...]
    kv = kv_ref[...].astype(F32)
    swapped = pltpu.roll(kv, HEAD, 1)
    kx_ref[0] = jnp.where(all_upper, 0.0, kv).astype(BF)
    kx_ref[1] = jnp.where(all_upper, swapped, 0.0).astype(BF)
    vx_ref[0] = jnp.where(all_upper, 0.0, swapped).astype(BF)
    vx_ref[1] = jnp.where(all_upper, kv, 0.0).astype(BF)
    lset_ref[...] = jnp.transpose(lse_ref[...])

    above = lax.broadcasted_iota(jnp.int32, (BLOCK, BLOCK), 0) <= lax.broadcasted_iota(
        jnp.int32, (BLOCK, BLOCK), 1
    )
    gx_ref[...] = jnp.zeros(gx_ref.shape, F32)
    for i in range(blocks):
        rows = slice(i * BLOCK, (i + 1) * BLOCK)
        seen = (i + 1) * BLOCK

        def pair(j, _, rows=rows, seen=seen, i=i):
            query = (slotq_ref[j, rows, :].astype(F32) * (HEAD**-0.5)).astype(BF)
            gslot = gslot_ref[j, rows, :]
            gq = jnp.zeros((BLOCK, LANES), F32)
            for h in range(2):
                keys = kx_ref[h, :seen, :]
                log = lset_ref[pl.ds(2 * j + h, 1), rows]
                scores = dot(keys, query, NT) - log
                last = jnp.where(above, scores[i * BLOCK :, :], NEG)
                scores = last if i == 0 else jnp.concatenate([scores[: i * BLOCK], last], axis=0)
                probs = jnp.exp(scores)
                gprob = dot(vx_ref[h, :seen, :], gslot, NT)
                inner = lset_ref[pl.ds(A_TOP + 2 * j + h, 1), rows]
                gs = (probs * (gprob - inner)).astype(BF)
                gq = gq + dot(gs, keys, TN)
                gx_ref[0, h, :seen, :] += dot(gs, query)
                gx_ref[1, h, :seen, :] += dot(probs.astype(BF), gslot)
            gq_ref[j, rows, :] = gq * (HEAD**-0.5)
            return 0

        lax.fori_loop(0, A_TOP // 2, pair, 0)

    def input_back(b, gkv_sum):
        rows = pl.ds(b * BLOCK, BLOCK)
        meta = meta_ref[rows, :]
        pairs = [gq_ref[j, rows, :] for j in range(A_TOP // 2)]

        def store(p, block):
            wide_ref[:, p * LANES : (p + 1) * LANES] = block

        spread_heads(pairs, meta, lane, lane_half, store)
        gkeys = gx_ref[0, 0, rows, :] + pltpu.roll(gx_ref[0, 1, rows, :], HEAD, 1)
        gvals = pltpu.roll(gx_ref[1, 0, rows, :], HEAD, 1) + gx_ref[1, 1, rows, :]
        gkv = jnp.where(upper, gvals, gkeys).astype(BF)
        gla_high, gla_low = split_two(gla_ref[rows, :])
        grad = dot(wide_ref[...], w_ref[:, :WIDTH], NT)
        grad = grad + dot(gkv, w_ref[:, KV_AT:RV_AT], NT)
        grad = grad + dot(gla_high, low_t) + dot(gla_low, low_t)
        hat, inv = norm_stats(tok_ref[rows, :].astype(F32))
        normed = (hat * gain_one + shift_one).astype(BF)
        acc_ref[...] += dot(normed, wide_ref[...], TN)
        rv_ref[...] += dot(normed, gla_high, TN) + dot(normed, gla_low, TN)
        vec_ref[0:1, :] += jnp.sum(grad * hat, axis=0, keepdims=True)
        vec_ref[1:2, :] += jnp.sum(grad, axis=0, keepdims=True)
        gin_ref[rows, :] = (gh_ref[rows, :] + norm_back(grad, hat, inv, gain_one)).astype(BF)
        return gkv_sum + dot(normed, gkv, TN)

    gkv_sum = lax.fori_loop(0, blocks, input_back, jnp.zeros((D, LANES), F32))
    store_grads(pack_ref, acc_ref[...].astype(BF), 0)
    store_grads(pack_ref, gkv_sum.astype(BF), WIDTH)
    turned = pltpu.roll(jnp.transpose(vec_ref[...]), first, 1)
    tail = jnp.where(lane_ids(D) < first, rv_ref[...], turned)
    store_grads(pack_ref, tail.astype(BF), WIDTH + LANES)


VMEM_LIMIT = 60 * 1024 * 1024
VMEM_ALL = 67043328


def whole(shape, dtype):
    return jax.ShapeDtypeStruct(shape, dtype)


def in_vmem(count):
    return [pl.BlockSpec(memory_space=pltpu.VMEM)] * count


def call(kernel, inputs, outs, scratch=(), limit=VMEM_LIMIT):
    return pl.pallas_call(
        kernel,
        out_shape=outs,
        in_specs=in_vmem(len(inputs)),
        out_specs=in_vmem(len(outs)),
        scratch_shapes=list(scratch),
        compiler_params=pltpu.CompilerParams(vmem_limit_bytes=limit),
    )(*inputs)


def constant_spec(shape, middle=0):
    return pl.BlockSpec(shape, lambda s: (0, middle, 0), pipeline_mode=pl.Buffered(1))


def gather_pieces(pack, shape):
    groups, experts, _ = shape
    if experts != 8 or groups != 4:
        own = lax.all_gather(pack, "dp", axis=0, tiled=False)
        every = lax.all_gather(own, "fsdp", axis=0, tiled=False)
        return [every.transpose(1, 0, 2, 3).reshape(D, PACK)]

    own = [pack]
    for d in range(1, groups):
        pairs = [((i + d) % groups, i) for i in range(groups)]
        own.append(lax.ppermute(pack, "dp", pairs))
    own = jnp.stack(own)

    def swap(values, m):
        return lax.ppermute(values, "fsdp", [(i, i ^ m) for i in range(experts)])

    along = swap(own, 2)
    across = swap(own, 4)
    low = swap(along[: groups // 2], 4)
    high = swap(across[groups // 2 :], 2)
    return [
        own,
        swap(own, 1),
        along,
        swap(along, 1),
        across,
        swap(across, 1),
        low,
        high,
        swap(low, 1),
        swap(high, 1),
    ]


def on_device(
    tokens,
    halt_in,
    depths,
    attn_routes,
    ffn_routes,
    w_query,
    w_out,
    w_kv,
    router,
    vectors,
    w_up,
    w_down,
    cot_out,
    cot_halt,
):
    tok = tokens.shape[0]
    groups, experts = lax.axis_size("dp"), lax.axis_size("fsdp")
    capacity = 2 * F_TOP * tok // experts
    slice_width = w_up.shape[2]
    shard = w_query.shape[0]
    slots = experts * capacity

    tail = jnp.concatenate([router, vectors.T], axis=1)
    tail = jnp.pad(tail, ((0, 0), (0, LANES - tail.shape[1])))
    pack = jnp.concatenate([w_query, w_out.T, w_kv, tail], axis=1)
    shape = (groups, experts, shard)
    pieces = gather_pieces(pack, shape)
    joined = slice_width == D
    if joined:
        expert_pack = jnp.concatenate([w_up[0], w_down[0]], axis=0)
        whole_up = whole_down = lax.all_gather(expert_pack, "dp", axis=0, tiled=False)
    else:
        whole_up = lax.all_gather(w_up[0], "dp", axis=0, tiled=False)
        whole_down = lax.all_gather(w_down[0], "dp", axis=0, tiled=False)

    meta = jnp.concatenate([attn_routes, ffn_routes, depths[:, None], depths[:, None]], axis=1)
    scal = jnp.stack([halt_in, cot_halt], axis=1)
    half = capacity // HALVES
    half_slots = slots // HALVES

    rank, rank_t, place, scal = call(
        partial(ranks_kernel, capacity),
        (meta, scal),
        (
            whole((tok, LANES), F32),
            whole((experts, tok), jnp.int32),
            whole((tok, LANES), jnp.int32),
            whole((tok, LANES), F32),
        ),
    )

    def gather_rows(rows, name, starts):
        ends = starts[1:] + (starts[0] + half,)
        shapes = [whole((experts, end - start, D), BF) for start, end in zip(starts, ends)]
        limit = VMEM_LIMIT if name == "cot_slots" else VMEM_ALL
        return call(partial(gather_kernel, experts, starts), (rank_t, rows), shapes, limit=limit)

    cot_slots = gather_rows(cot_out, "cot_slots", (0,))

    def exchange(values):
        came = lax.all_to_all(values, "fsdp", split_axis=0, concat_axis=0, tiled=True)
        return came

    *pieces, cot_first = lax.optimization_barrier((*pieces, cot_slots[0]))
    owned_cot = [exchange(cot_first)]

    attend_outs = (
        whole((D, PACK), BF),
        whole((2, tok, LANES), BF),
        whole((tok, LANES), BF),
        whole((2, tok, LANES), F32),
        whole((tok, LANES), F32),
        whole((tok, LANES), F32),
        whole((tok, WIDTH), BF),
        whole((tok, D), F32),
        whole((tok, LANES), F32),
        whole((tok, D), BF),
        whole((experts, half, D), BF),
    )
    weights, slotq, kv, so, lse, gates, mixed, hidden, fgate, normed_two, sent = pl.pallas_call(
        partial(attend_kernel, experts, shape),
        name="attend",
        out_shape=attend_outs,
        in_specs=in_vmem(3 + len(pieces)),
        out_specs=[pl.BlockSpec(memory_space=pl.ANY)] * len(attend_outs),
        scratch_shapes=[pltpu.VMEM(out.shape, out.dtype) for out in attend_outs]
        + [
            pltpu.VMEM((2, tok, LANES), BF),
            pltpu.VMEM((2, tok, LANES), BF),
            pltpu.SemaphoreType.DMA((len(attend_outs), max(tok // BLOCK, experts // 2))),
        ],
        compiler_params=pltpu.CompilerParams(vmem_limit_bytes=VMEM_ALL),
    )(tokens, meta, rank_t, *pieces)
    n2_slots = [sent, *gather_rows(normed_two, "dispatch_1", (half,))]
    n2_slots[0], owned_cot[0] = lax.optimization_barrier((n2_slots[0], owned_cot[0]))
    cot_slots += gather_rows(cot_out, "cot_late", (half, half + half // 2))

    up_spec = constant_spec((groups, D, slice_width))
    down_spec = constant_spec((groups, slice_width, D), 1 if joined else 0)
    params = pltpu.CompilerParams(vmem_limit_bytes=VMEM_ALL)
    wide = whole((groups, half_slots, slice_width), BF)
    narrow = whole((half_slots, D), BF)
    step_rows = max(half, min(512, half_slots))
    step_spec = pl.BlockSpec((step_rows, D), lambda s: (s, 0))
    step_wide = pl.BlockSpec((groups, step_rows, slice_width), lambda s: (0, s, 0))

    owned = []
    for h in range(HALVES):
        owned.append(exchange(n2_slots[h]).reshape(half_slots, D))
        if h + 1 < HALVES:
            n2_slots[h + 1], owned[h] = lax.optimization_barrier((n2_slots[h + 1], owned[h]))
    outs, acts, slopes = [], [], []
    for h in range(HALVES):
        out, act, slope = pl.pallas_call(
            partial(expert_kernel, groups),
            grid=(half_slots // step_rows,),
            out_shape=(narrow, wide, wide),
            in_specs=[step_spec, up_spec, down_spec],
            out_specs=[step_spec, step_wide, step_wide],
            scratch_shapes=[pltpu.VMEM((step_rows, D), F32)],
            compiler_params=params,
        )(owned[h], whole_up, whole_down)
        outs.append(out)
        acts.append(act)
        slopes.append(slope)
    back = []
    for h in range(HALVES):
        back.append(exchange(outs[h].reshape(experts, half, D)).reshape(half_slots, D))

    tail_spec = pl.BlockSpec((D, LANES), lambda s: (0, RV_AT // LANES))
    full = pl.BlockSpec(memory_space=pltpu.VMEM)
    sums = pl.pallas_call(
        partial(combine_first_kernel, experts),
        name="combine_first",
        grid=(1,),
        out_shape=(
            whole((tok, D), F32),
            whole((tok, LANES), F32),
            whole((3, max(16, experts), tok), BF),
        ),
        in_specs=[full, full, tail_spec, full, full, full],
        out_specs=[full] * 3,
        scratch_shapes=[pltpu.VMEM((tok, LANES), F32)],
        compiler_params=params,
    )(back[0], place, weights, meta, fgate, cot_out)
    back[1], cot_second = lax.optimization_barrier((back[1], cot_slots[1]))
    owned_cot.append(exchange(cot_second))

    def tokens_of(width, count=BLOCK):
        return pl.BlockSpec((count, width), lambda b: (b, 0))

    block_out, halt_wide, halt_slope, glf, halt_grad, ab = pl.pallas_call(
        partial(combine_kernel, experts, capacity),
        name="combine",
        grid=(tok // BLOCK,),
        out_shape=(
            whole((tok, D), BF),
            whole((tok, LANES), F32),
            whole((tok, LANES), F32),
            whole((tok, LANES), F32),
            whole((8, D), F32),
            whole((experts, 8, capacity), BF),
        ),
        in_specs=[
            full,
            tokens_of(D),
            tokens_of(LANES),
            full,
            tokens_of(LANES),
            full,
            tokens_of(D),
            tail_spec,
            tokens_of(meta.shape[1]),
            tokens_of(LANES),
            tokens_of(LANES),
            tokens_of(D),
        ],
        out_specs=[tokens_of(D)] + [tokens_of(LANES)] * 3 + [full] * 2,
        scratch_shapes=[pltpu.VMEM((tok, LANES), F32)],
        compiler_params=params,
    )(back[1], *sums, place, rank_t, hidden, weights, meta, fgate, scal, cot_out)
    halt_out = halt_wide[:, 0]
    ab, owned_cot[1] = lax.optimization_barrier((ab, owned_cot[1]))
    owned_ab = exchange(ab)
    owned_ab, cot_third = lax.optimization_barrier((owned_ab, cot_slots[2]))
    owned_cot.append(exchange(cot_third))
    cot_parts = [owned_cot[:1], owned_cot[1:]]

    together = step_rows // half if half % LANES == 0 else 1
    row_spec = pl.BlockSpec((together * half, D), lambda s: (s, 0))
    wide_spec = pl.BlockSpec((groups, together * half, slice_width), lambda s: (0, s, 0))
    gys, gpres, rows_back = [], [], []
    for h in range(HALVES):
        gpre, gy, owned_rows = pl.pallas_call(
            partial(data_back_kernel, experts, groups, h),
            grid=(experts // together,),
            out_shape=(wide, narrow, narrow),
            in_specs=[
                *(pl.BlockSpec((together * part.shape[1], D), lambda s: (s, 0)) for part in cot_parts[h]),
                pl.BlockSpec((together, 8, capacity), lambda s: (s, 0, 0)),
                tail_spec,
                wide_spec,
                up_spec,
                down_spec,
            ],
            out_specs=[wide_spec, row_spec, row_spec],
            compiler_params=params,
        )(
            *(part.reshape(-1, D) for part in cot_parts[h]),
            owned_ab,
            weights,
            slopes[h],
            whole_up,
            whole_down,
        )
        gys.append(gy)
        gpres.append(gpre)
        rows_back.append(exchange(owned_rows.reshape(experts, half, D)))

    steps = half_slots // step_rows
    specs, inputs = [], []
    for h in range(HALVES):

        def at(s, h=h):
            return jnp.clip(s - h * steps, 0, steps - 1)

        narrow_at = pl.BlockSpec((step_rows, D), lambda s, at=at: (at(s), 0))
        wide_at = pl.BlockSpec((groups, step_rows, slice_width), lambda s, at=at: (0, at(s), 0))
        specs += [narrow_at, narrow_at, wide_at, wide_at]
        inputs += [owned[h], gys[h], gpres[h], acts[h]]
    if joined:
        grad_shapes = [(groups, 2 * D, D)]
    else:
        grad_shapes = [(groups, D, slice_width), (groups, slice_width, D)]
    expert_grads = pl.pallas_call(
        partial(weight_back_kernel, groups, steps, joined),
        name="weight_back",
        grid=(HALVES * steps,),
        out_shape=[whole(g, BF) for g in grad_shapes],
        in_specs=specs,
        out_specs=[constant_spec(g) for g in grad_shapes],
        scratch_shapes=[pltpu.VMEM((groups, D, slice_width), F32)] * 2,
        compiler_params=params,
    )(*inputs)
    expert_grads = [
        lax.psum_scatter(g, "dp", scatter_dimension=0, tiled=True) for g in expert_grads
    ]
    expert_grads = [g.astype(F32) for g in expert_grads]
    if joined:
        part_up, part_down = expert_grads[0][:, :D], expert_grads[0][:, D:]
    else:
        part_up, part_down = expert_grads

    ordered = shard % 16 == 0

    def grads_shape(width):
        return whole((experts, groups, shard, width) if ordered else (D, width), BF)

    wide_block = BLOCK
    pair_spec = pl.BlockSpec((2, wide_block, LANES), lambda b: (0, b, 0))
    lanes_spec = tokens_of(LANES, wide_block)
    grad_out, gh, gslot, gla, logs, rv, vec = pl.pallas_call(
        partial(hidden_back_kernel, experts, capacity),
        name="hidden_back",
        grid=(tok // wide_block,),
        out_shape=(
            grads_shape(WIDTH),
            whole((tok, D), F32),
            whole((2, tok, LANES), BF),
            whole((tok, LANES), F32),
            whole((tok, LANES), F32),
            whole((D, LANES), F32),
            whole((8, D), F32),
        ),
        in_specs=[
            full,
            full,
            lanes_spec,
            tokens_of(D, wide_block),
            pl.BlockSpec((D, WIDTH), lambda b: (0, 1), pipeline_mode=pl.Buffered(1)),
            tail_spec,
            tokens_of(meta.shape[1], wide_block),
            tokens_of(D, wide_block),
            lanes_spec,
            lanes_spec,
            tokens_of(WIDTH, wide_block),
            pair_spec,
            lanes_spec,
            lanes_spec,
        ],
        out_specs=[full, tokens_of(D, wide_block), pair_spec, lanes_spec, lanes_spec, full, full],
        scratch_shapes=[pltpu.VMEM((D, WIDTH), F32)],
        compiler_params=pltpu.CompilerParams(vmem_limit_bytes=VMEM_LIMIT),
    )(
        *rows_back,
        rank,
        hidden,
        weights,
        weights,
        meta,
        cot_out,
        halt_slope,
        glf,
        mixed,
        so,
        gates,
        lse,
    )

    def reduced(sent):
        if not ordered:
            sent = sent.reshape(groups, experts, shard, sent.shape[1]).transpose(1, 0, 2, 3)
        return jnp.sum(exchange(sent).astype(F32), axis=0).astype(BF)

    part_out = reduced(grad_out)
    paired = ordered and experts == 8
    last_shape = grads_shape(WIDTH + 2 * LANES)
    if paired:
        last_shape = whole((2, experts // 2, groups, shard, WIDTH + 2 * LANES), BF)

    def reduced_last(grads):
        if not paired:
            return reduced(grads)
        other = lax.ppermute(grads, "fsdp", [(i, i ^ 1) for i in range(experts)])
        chip = (grads[0].astype(F32) + other[1].astype(F32)).astype(BF)
        same = [list(range(c, experts, 2)) for c in range(2)]
        came = lax.all_to_all(
            chip, "fsdp", split_axis=0, concat_axis=0, tiled=True, axis_index_groups=same
        )
        return jnp.sum(came.astype(F32), axis=0).astype(BF)

    grad_in, grads = call(
        partial(input_back_kernel, experts),
        (tokens, weights, meta, gh, gslot, gla, rv, vec, halt_grad, logs, slotq, kv),
        (whole((tok, D), BF), last_shape),
        (
            pltpu.VMEM((2, 2, tok, LANES), F32),
            pltpu.VMEM((BLOCK, WIDTH), BF),
            pltpu.VMEM((D, WIDTH), F32),
            pltpu.VMEM((D, LANES), F32),
            pltpu.VMEM((LANES, D), F32),
            pltpu.VMEM((2, tok, LANES), BF),
            pltpu.VMEM((2, tok, LANES), BF),
            pltpu.VMEM((LANES, tok), F32),
            pltpu.VMEM((2, tok, LANES), F32),
        ),
    )
    part = jnp.concatenate([reduced_last(grads), part_out], axis=2)
    came = lax.all_to_all(part, "dp", split_axis=0, concat_axis=0, tiled=True)
    total = jnp.sum(came.astype(F32), axis=0)
    kv_end = WIDTH + LANES
    router_end = kv_end + A_EXP + experts
    return (
        block_out,
        halt_out,
        grad_in,
        total[:, :WIDTH],
        total[:, WIDTH + 2 * LANES :].T,
        total[:, WIDTH:kv_end],
        total[:, kv_end:router_end],
        total[:, router_end : router_end + 5].T,
        part_up,
        part_down,
    )


def solution(mesh):
    both = ("dp", "fsdp")
    placed = (
        P(both, None),
        P(both),
        P(both),
        P(both, None),
        P(both, None),
        P(both, None),
        P(None, both),
        P(both, None),
        P(both, None),
        P(None, both),
        P("fsdp", None, "dp"),
        P("fsdp", "dp", None),
        P(both, None),
        P(both),
    )

    return jax.shard_map(
        on_device,
        mesh=mesh,
        in_specs=placed,
        out_specs=(
            P(both, None),
            P(both),
            P(both, None),
            P(both, None),
            P(None, both),
            P(both, None),
            P(both, None),
            P(None, both),
            P("fsdp", None, "dp"),
            P("fsdp", "dp", None),
        ),
        check_vma=False,
    )
```

profile of v0, /device:TPU:0, one launch (start us, length us, event | category | flops | bytes accessed | tf_op | source)
XLA Modules:
  0.0 492.5 jit_solution(16474156334806254434)
XLA Ops:
  27.9 5.4 %collective-permute-done.6.refs_7_ = bf16[4,16,3328]{2,1,0:T(8,128)(2,1)S(1)} collective-permute-done((bf16[4,16,3328]{2,1,0:T(8,128)(2,1)S(1)}, bf16[4,16,3328]{2,1,0:T(8,128)(2,1)S(1)}, u32[]{:S(2)}, u32[]{:S(2)}) %collective-permute-start.6) | collective-permute-done | bytes 426016 | tf_op jit(solution)/shard_map/ppermute | solution.py:833
  43.0 5.3 %shard_map.213 = (f32[1024,128]{1,0:T(8,128)}, s32[8,1024]{1,0:T(8,128)}, s32[1024,128]{1,0:T(8,128)}, f32[1024,128]{1,0:T(8,128)}) custom-call(s32[1024,8]{1,0:T(8,128)} %copy.54.meta_ref.refs_1_, f32[1024,2]{1,0:T(8,128)} %copy.55.pair_ref), custom_call_target="tpu_custom_call" | custom-call | tf_op jit(solution)/shard_map/pallas_call | solution.py:805
  48.3 5.4 %shard_map.214 = bf16[8,256,512]{2,1,0:T(8,128)(2,1)} custom-call(s32[8,1024]{1,0:T(8,128)} %get-tuple-element.78.rank_t_ref.refs_2_, bf16[1024,512]{1,0:T(8,128)(2,1)} %cot_ref.5), custom_call_target="tpu_custom_call" | custom-call | tf_op jit(solution)/shard_map/pallas_call | solution.py:805
  59.8 26.8 %attend.1 = (bf16[512,3328]{1,0:T(8,128)(2,1)}, bf16[2,1024,128]{2,1,0:T(8,128)(2,1)}, bf16[1024,128]{1,0:T(8,128)(2,1)}, f32[2,1024,128]{2,1,0:T(8,128)}, f32[1...) custom-call(bf16[1024,512]{1,0:T(8,128)(2,1)} %tok_ref.1, ...), custom_call_target="tpu_custom_call" | custom-call | tf_op jit(solution)/shard_map/attend/pallas_call | solution.py:933
  91.0 5.4 %shard_map.215 = bf16[8,256,512]{2,1,0:T(8,128)(2,1)} custom-call(s32[8,1024]{1,0:T(8,128)} %get-tuple-element.78.rank_t_ref.refs_2_, bf16[1024,512]{1,0:T(8,128)(2,1)} %get-tuple-element.89.rows_ref), custom_call_target="tpu_custom_call" | custom-call | tf_op jit(solution)/shard_map/pallas_call | solution.py:805
  96.4 21.2 %all-to-all-done.1 = bf16[8,256,512]{2,1,0:T(8,128)(2,1)} async-done(((bf16[8,256,512]{2,1,0:T(8,128)(2,1)}), bf16[8,256,512]{2,1,0:T(8,128)(2,1)}, u32[]{:S(2)}, u32[]{:S(2)}) %all-to-all-start.1) | async-done | bytes 2097184 | tf_op jit(solution)/shard_map/all_to_all | solution.py:914
  122.5 26.6 %all-to-all-done.2 = bf16[8,256,512]{2,1,0:T(8,128)(2,1)} async-done(((bf16[8,256,512]{2,1,0:T(8,128)(2,1)}), bf16[8,256,512]{2,1,0:T(8,128)(2,1)}, u32[]{:S(2)}, u32[]{:S(2)}) %all-to-all-start.2) | async-done | bytes 2097184 | tf_op jit(solution)/shard_map/all_to_all | solution.py:914
  149.1 26.5 %shard_map.216 = (bf16[2048,512]{1,0:T(8,128)(2,1)}, bf16[4,2048,512]{2,1,0:T(8,128)(2,1)}, bf16[4,2048,512]{2,1,0:T(8,128)(2,1)}) custom-call(bf16[2048,512]{1,0:T(8,128)(2,1)} %bitcast.10.x_ref.refs_4_, bf16[4,1024,512]{2,1,0:T(8,128)(2,1)} %bitcast.30, bf16[4,1024,512]{2,1,0:T(8,128)(2,1)} %bitcast.31), custom_call_target="tpu_custom_call" | custom-call | tf_op jit(solution)/shard_map/pallas_call | solution.py:967
  179.9 26.3 %shard_map.218 = (bf16[2048,512]{1,0:T(8,128)(2,1)}, bf16[4,2048,512]{2,1,0:T(8,128)(2,1)}, bf16[4,2048,512]{2,1,0:T(8,128)(2,1)}) custom-call(bf16[2048,512]{1,0:T(8,128)(2,1)} %bitcast.9.x_ref.refs_0_, bf16[4,1024,512]{2,1,0:T(8,128)(2,1)} %bitcast.32, bf16[4,1024,512]{2,1,0:T(8,128)(2,1)} %bitcast.33), custom_call_target="tpu_custom_call" | custom-call | tf_op jit(solution)/shard_map/pallas_call | solution.py:967
  210.9 5.4 %shard_map.217 = (bf16[8,128,512]{2,1,0:T(8,128)(2,1)}, bf16[8,128,512]{2,1,0:T(8,128)(2,1)}) custom-call(s32[8,1024]{1,0:T(8,128)} %get-tuple-element.78.rank_t_ref.refs_2_, bf16[1024,512]{1,0:T(8,128)(2,1)} %cot_ref.5), custom_call_target="tpu_custom_call" | custom-call | tf_op jit(solution)/shard_map/pallas_call | solution.py:805
  216.2 21.3 %all-to-all-done.4 = bf16[8,256,512]{2,1,0:T(8,128)(2,1)} async-done(((bf16[8,256,512]{2,1,0:T(8,128)(2,1)}), bf16[8,256,512]{2,1,0:T(8,128)(2,1)}, u32[]{:S(2)}, u32[]{:S(2)}) %all-to-all-start.4) | async-done | bytes 2097184 | tf_op jit(solution)/shard_map/all_to_all | solution.py:914
  241.8 9.8 %combine_first.1 = (f32[1024,512]{1,0:T(8,128)}, f32[1024,128]{1,0:T(8,128)}, bf16[3,16,1024]{2,1,0:T(8,128)(2,1)}) custom-call(bf16[2048,512]{1,0:T(8,128)(2,1)} %bitcast.17.back_ref, s32[1024,128]{1,0:T(8,128)} %get-tuple-element.99.place_ref, bf16[512,3328]{1,0:T(8,128)(2,1)} %get-tuple-element.100.tail_ref.refs_2_.refs_3_.w_ref, ...), custom_call_target="tpu_custom_call" | custom-call | tf_op jit(solution)/shard_map/combine_first/pallas_call | solution.py:985
  251.6 15.7 %combine.1 = (bf16[1024,512]{1,0:T(8,128)(2,1)}, f32[1024,128]{1,0:T(8,128)}, f32[1024,128]{1,0:T(8,128)}, f32[1024,128]{1,0:T(8,128)}, f32[8,512]{1,0:T(8,128)}, /*index=5*/bf16[8,8,512]{2,1,0:T(8,128)(2,1)}) custom-call(bf16[2048,512]{1,0:T(8,128)(2,1)} %bitcast.15.back_ref, f32[1024,512]{1,0:T(8,128)} %get-tuple-element.102.branch_ref, ...), custom_call_target="tpu_custom_call" | custom-call | tf_op jit(solution)/shard_map/combine/pallas_call | solution.py:1005
  267.3 9.2 %all_to_all.65.refs_1_.refs_2_ = bf16[8,8,512]{2,1,0:T(8,128)(2,1)} all-to-all(bf16[8,8,512]{2,1,0:T(8,128)(2,1)} %get-tuple-element.112), channel_id=1, replica_groups=mesh['dp'=4,'fsdp'=8] {'fsdp'}, dimensions={0} | all-to-all | bytes 131072 | tf_op jit(solution)/shard_map/all_to_all | solution.py:914
  281.0 15.8 %shard_map.219 = (bf16[4,2048,512]{2,1,0:T(8,128)(2,1)}, bf16[2048,512]{1,0:T(8,128)(2,1)}, bf16[2048,512]{1,0:T(8,128)(2,1)}) custom-call(bf16[2048,512]{1,0:T(8,128)(2,1)} %bitcast.18.refs_0_, bf16[8,8,512]{2,1,0:T(8,128)(2,1)} %all_to_all.65.refs_1_.refs_2_, bf16[512,3328]{1,0:T(8,128)(2,1)} %get-tuple-element.100.tail_ref.refs_2_.refs_3_.w_ref, ...), custom_call_target="tpu_custom_call" | custom-call | tf_op jit(solution)/shard_map/pallas_call | solution.py:1047
  301.2 15.8 %shard_map.220 = (bf16[4,2048,512]{2,1,0:T(8,128)(2,1)}, bf16[2048,512]{1,0:T(8,128)(2,1)}, bf16[2048,512]{1,0:T(8,128)(2,1)}) custom-call(bf16[1024,512]{1,0:T(8,128)(2,1)} %bitcast.20.refs_0_, bf16[1024,512]{1,0:T(8,128)(2,1)} %bitcast.21.refs_1_, bf16[8,8,512]{2,1,0:T(8,128)(2,1)} %all_to_all.65.refs_1_.refs_2_, ...), custom_call_target="tpu_custom_call" | custom-call | tf_op jit(solution)/shard_map/pallas_call | solution.py:1047
  316.9 27.2 %weight_back.1 = bf16[4,1024,512]{2,1,0:T(8,128)(2,1)} custom-call(bf16[2048,512]{1,0:T(8,128)(2,1)} %bitcast.9.x_ref.refs_0_, bf16[2048,512]{1,0:T(8,128)(2,1)} %get-tuple-element.140.refs_1_, bf16[4,2048,512]{2,1,0:T(8,128)(2,1)} %get-tuple-element.141.refs_2_, bf16[4,2048,512]{2,1,0:T(8,128)(2,1)} %get-tuple-element.142.refs_3_, ...), custom_call_target="tpu_custom_call" | custom-call | tf_op jit(solution)/shard_map/weight_back/pallas_call | solution.py:1088
  345.7 30.8 %all_to_all.66.second_ref = bf16[8,256,512]{2,1,0:T(8,128)(2,1)} all-to-all(bf16[8,256,512]{2,1,0:T(8,128)(2,1)S(1)} %bitcast.39), channel_id=1, replica_groups=mesh['dp'=4,'fsdp'=8] {'fsdp'}, dimensions={0} | all-to-all | bytes 4194304 | tf_op jit(solution)/shard_map/all_to_all | solution.py:914
  376.5 21.3 %hidden_back.1 = (bf16[8,4,16,1536]{3,2,1,0:T(8,128)(2,1)}, f32[1024,512]{1,0:T(8,128)}, bf16[2,1024,128]{2,1,0:T(8,128)(2,1)}, f32[1024,128]{1,0:T(8,128)}, f32...) custom-call(bf16[8,256,512]{2,1,0:T(8,128)(2,1)} %all-to-all-done.7.first_ref, ...), custom_call_target="tpu_custom_call" | custom-call | tf_op jit(solution)/shard_map/hidden_back/pallas_call | solution.py:1115
  397.8 24.4 %shard_map.221 = (bf16[1024,512]{1,0:T(8,128)(2,1)}, bf16[2,4,4,16,1792]{4,3,2,1,0:T(8,128)(2,1)}) custom-call(bf16[1024,512]{1,0:T(8,128)(2,1)} %tok_ref.1, bf16[512,3328]{1,0:T(8,128)(2,1)} %get-tuple-element.100.tail_ref.refs_2_.refs_3_.w_ref, s32[1024,8]{1,0:T(8,128)} %copy.54.meta_ref.refs_1_, f32[1024,512]{1,0:T(8,128)} %get-tuple-element.128.gh_ref, ...), custom_call_target="tpu_custom_call" | custom-call | tf_op jit(solution)/shard_map/pallas_call | solution.py:805
  428.7 18.2 %all-to-all-done.11 = bf16[8,4,16,1536]{3,2,1,0:T(8,128)(2,1)S(1)} async-done(((bf16[8,4,16,1536]{3,2,1,0:T(8,128)(2,1)}), bf16[8,4,16,1536]{3,2,1,0:T(8,128)(2,1)S(1)}, u32[]{:S(2)}, u32[]{:S(2)}) %all-to-all-start.11) | async-done | bytes 1572896 | tf_op jit(solution)/shard_map/all_to_all | solution.py:914
  450.7 11.2 %all-to-all-done.10 = bf16[4,4,16,1792]{3,2,1,0:T(8,128)(2,1)S(1)} async-done(((bf16[4,4,16,1792]{3,2,1,0:T(8,128)(2,1)}), bf16[4,4,16,1792]{3,2,1,0:T(8,128)(2,1)S(1)}, u32[]{:S(2)}, u32[]{:S(2)}) %all-to-all-start.10) | async-done | bytes 917536 | tf_op jit(solution)/shard_map/all_to_all | solution.py:1180
  462.9 6.2 %all-to-all-start.12 = ((bf16[4,16,3328]{2,1,0:T(8,128)(2,1)}), bf16[4,16,3328]{2,1,0:T(8,128)(2,1)S(1)}, u32[]{:S(2)}, u32[]{:S(2)}) async-start(bf16[4,16,3328]{2,1,0:T(8,128)(2,1)} %pad_maximum_fusion.2), calls=%async_computation.12 | async-start | bytes 851968 | tf_op jit(solution)/shard_map/all_to_all | solution.py:1202
  469.9 10.1 %all-to-all-done.12 = bf16[4,16,3328]{2,1,0:T(8,128)(2,1)S(1)} async-done(((bf16[4,16,3328]{2,1,0:T(8,128)(2,1)}), bf16[4,16,3328]{2,1,0:T(8,128)(2,1)S(1)}, u32[]{:S(2)}, u32[]{:S(2)}) %all-to-all-start.12) | async-done | bytes 426016 | tf_op jit(solution)/shard_map/all_to_all | solution.py:1202
  (105 shorter events, 86.6 us)
Async XLA Ops:
  7.2 115.3 %all-gather.3.cloned.1.call-start = ((), (), s32[]{:S(2)}) async-start(), calls=%async_computation.15 | async-start | bytes 5242880 | tf_op jit(solution)/shard_map/all_gather | solution.py:884
  9.6 11.1 %collective-permute-start.1 = (bf16[16,3328]{1,0:T(8,128)(2,1)S(1)}, bf16[16,3328]{1,0:T(8,128)(2,1)S(1)}, u32[]{:S(2)}, u32[]{:S(2)}) collective-permute-start(bf16[16,3328]{1,0:T(8,128)(2,1)S(1)} %get-tuple-element.191), channel_id=1, source_target_pairs={{16,0},{24,8},{0,16},{8,24},{17,1},{25,9},{1,17},{9,25},{18,2},{26... | collective-permute-start | bytes 319496 | tf_op jit(solution)/shard_map/ppermute | solution.py:829
  13.7 6.9 %collective-permute-start = (bf16[16,3328]{1,0:T(8,128)(2,1)S(1)}, bf16[16,3328]{1,0:T(8,128)(2,1)S(1)}, u32[]{:S(2)}, u32[]{:S(2)}) collective-permute-start(bf16[16,3328]{1,0:T(8,128)(2,1)S(1)} %get-tuple-element.191), channel_id=1, source_target_pairs={{8,0},{16,8},{24,16},{0,24},{9,1},{17,9},{25,17},{1,25},{10,2},{18... | collective-permute-start | bytes 319496 | tf_op jit(solution)/shard_map/ppermute | solution.py:829
  15.1 7.3 %collective-permute-start.2 = (bf16[16,3328]{1,0:T(8,128)(2,1)S(1)}, bf16[16,3328]{1,0:T(8,128)(2,1)S(1)}, u32[]{:S(2)}, u32[]{:S(2)}) collective-permute-start(bf16[16,3328]{1,0:T(8,128)(2,1)S(1)} %get-tuple-element.191), channel_id=1, source_target_pairs={{24,0},{0,8},{8,16},{16,24},{25,1},{1,9},{9,17},{17,25},{26,2},{2,... | collective-permute-start | bytes 319496 | tf_op jit(solution)/shard_map/ppermute | solution.py:829
  22.5 10.8 %collective-permute-start.6 = (bf16[4,16,3328]{2,1,0:T(8,128)(2,1)S(1)}, bf16[4,16,3328]{2,1,0:T(8,128)(2,1)S(1)}, u32[]{:S(2)}, u32[]{:S(2)}) collective-permute-start(bf16[4,16,3328]{2,1,0:T(8,128)(2,1)S(1)} %pad_maximum_fusion.1.refs_3_), channel_id=1, source_target_pairs={{0,4},{1,5},{2,6},{3,7},{4,0},{5,1},{6,2},{7,3},{8,12},{9,13},{10,... | collective-permute-start | bytes 1277960 | tf_op jit(solution)/shard_map/ppermute | solution.py:833
  24.1 10.8 %collective-permute-start.4 = (bf16[4,16,3328]{2,1,0:T(8,128)(2,1)S(1)}, bf16[4,16,3328]{2,1,0:T(8,128)(2,1)S(1)}, u32[]{:S(2)}, u32[]{:S(2)}) collective-permute-start(bf16[4,16,3328]{2,1,0:T(8,128)(2,1)S(1)} %pad_maximum_fusion.1.refs_3_), channel_id=1, source_target_pairs={{0,2},{1,3},{2,0},{3,1},{4,6},{5,7},{6,4},{7,5},{8,10},{9,11},{10,... | collective-permute-start | bytes 1277960 | tf_op jit(solution)/shard_map/ppermute | solution.py:833
  33.3 5.9 %collective-permute-start.9 = (bf16[2,16,3328]{2,1,0:T(8,128)(2,1)S(1)}, bf16[2,16,3328]{2,1,0:T(8,128)(2,1)S(1)}, u32[]{:S(2)}, u32[]{:S(2)}) collective-permute-start(bf16[2,16,3328]{2,1,0:T(8,128)(2,1)S(1)} %slice.49), channel_id=1, source_target_pairs={{0,2},{1,3},{2,0},{3,1},{4,6},{5,7},{6,4},{7,5},{8,10},{9,11},{10,... | collective-permute-start | bytes 638984 | tf_op jit(solution)/shard_map/ppermute | solution.py:833
  36.5 17.3 %collective-permute-start.3 = (bf16[4,16,3328]{2,1,0:T(8,128)(2,1)S(1)}, bf16[4,16,3328]{2,1,0:T(8,128)(2,1)S(1)}, u32[]{:S(2)}, u32[]{:S(2)}) collective-permute-start(bf16[4,16,3328]{2,1,0:T(8,128)(2,1)S(1)} %pad_maximum_fusion.1.refs_3_), channel_id=1, source_target_pairs={{0,1},{1,0},{2,3},{3,2},{4,5},{5,4},{6,7},{7,6},{8,9},{9,8},{10,11... | collective-permute-start | bytes 1277960 | tf_op jit(solution)/shard_map/ppermute | solution.py:833
  36.5 17.3 %collective-permute-start.7 = (bf16[4,16,3328]{2,1,0:T(8,128)(2,1)S(1)}, bf16[4,16,3328]{2,1,0:T(8,128)(2,1)S(1)}, u32[]{:S(2)}, u32[]{:S(2)}) collective-permute-start(bf16[4,16,3328]{2,1,0:T(8,128)(2,1)S(1)} %collective-permute-done.6.refs_7_), channel_id=1, source_target_pairs={{0,1},{1,0},{2,3},{3,2},{4,5},{5,4},{6,7},{7,6},{8,9},{9,8},{10,11... | collective-permute-start | bytes 1277960 | tf_op jit(solution)/shard_map/ppermute | solution.py:833
  37.0 16.9 %collective-permute-start.5 = (bf16[4,16,3328]{2,1,0:T(8,128)(2,1)S(1)}, bf16[4,16,3328]{2,1,0:T(8,128)(2,1)S(1)}, u32[]{:S(2)}, u32[]{:S(2)}) collective-permute-start(bf16[4,16,3328]{2,1,0:T(8,128)(2,1)S(1)} %collective-permute-done.4.refs_5_), channel_id=1, source_target_pairs={{0,1},{1,0},{2,3},{3,2},{4,5},{5,4},{6,7},{7,6},{8,9},{9,8},{10,11... | collective-permute-start | bytes 1277960 | tf_op jit(solution)/shard_map/ppermute | solution.py:833
  39.2 14.6 %collective-permute-start.11 = (bf16[2,16,3328]{2,1,0:T(8,128)(2,1)S(1)}, bf16[2,16,3328]{2,1,0:T(8,128)(2,1)S(1)}, u32[]{:S(2)}, u32[]{:S(2)}) collective-permute-start(bf16[2,16,3328]{2,1,0:T(8,128)(2,1)S(1)} %collective-permute-done.9.refs_10_), channel_id=1, source_target_pairs={{0,1},{1,0},{2,3},{3,2},{4,5},{5,4},{6,7},{7,6},{8,9},{9,8},{10,11... | collective-permute-start | bytes 638984 | tf_op jit(solution)/shard_map/ppermute | solution.py:833
  40.9 13.0 %collective-permute-start.10 = (bf16[2,16,3328]{2,1,0:T(8,128)(2,1)S(1)}, bf16[2,16,3328]{2,1,0:T(8,128)(2,1)S(1)}, u32[]{:S(2)}, u32[]{:S(2)}) collective-permute-start(bf16[2,16,3328]{2,1,0:T(8,128)(2,1)S(1)} %collective-permute-done.8.refs_9_), channel_id=1, source_target_pairs={{0,1},{1,0},{2,3},{3,2},{4,5},{5,4},{6,7},{7,6},{8,9},{9,8},{10,11... | collective-permute-start | bytes 638984 | tf_op jit(solution)/shard_map/ppermute | solution.py:833
  55.5 31.1 %all-to-all-start = ((bf16[8,256,512]{2,1,0:T(8,128)(2,1)}), bf16[8,256,512]{2,1,0:T(8,128)(2,1)}, u32[]{:S(2)}, u32[]{:S(2)}) async-start(bf16[8,256,512]{2,1,0:T(8,128)(2,1)} %shard_map.214), calls=%async_computation | async-start | bytes 4194304 | tf_op jit(solution)/shard_map/all_to_all | solution.py:914
  86.6 31.0 %all-to-all-start.1 = ((bf16[8,256,512]{2,1,0:T(8,128)(2,1)}), bf16[8,256,512]{2,1,0:T(8,128)(2,1)}, u32[]{:S(2)}, u32[]{:S(2)}) async-start(bf16[8,256,512]{2,1,0:T(8,128)(2,1)} %get-tuple-element.92), calls=%async_computation.1 | async-start | bytes 4194304 | tf_op jit(solution)/shard_map/all_to_all | solution.py:914
  117.6 31.5 %all-to-all-start.2 = ((bf16[8,256,512]{2,1,0:T(8,128)(2,1)}), bf16[8,256,512]{2,1,0:T(8,128)(2,1)}, u32[]{:S(2)}, u32[]{:S(2)}) async-start(bf16[8,256,512]{2,1,0:T(8,128)(2,1)} %shard_map.215), calls=%async_computation.2 | async-start | bytes 4194304 | tf_op jit(solution)/shard_map/all_to_all | solution.py:914
  175.5 31.0 %all-to-all-start.3 = ((bf16[8,256,512]{2,1,0:T(8,128)(2,1)}), bf16[8,256,512]{2,1,0:T(8,128)(2,1)}, u32[]{:S(2)}, u32[]{:S(2)}) async-start(bf16[8,256,512]{2,1,0:T(8,128)(2,1)} %bitcast.41), calls=%async_computation.3 | async-start | bytes 4194304 | tf_op jit(solution)/shard_map/all_to_all | solution.py:914
  206.5 31.0 %all-to-all-start.4 = ((bf16[8,256,512]{2,1,0:T(8,128)(2,1)}), bf16[8,256,512]{2,1,0:T(8,128)(2,1)}, u32[]{:S(2)}, u32[]{:S(2)}) async-start(bf16[8,256,512]{2,1,0:T(8,128)(2,1)} %bitcast.40), calls=%async_computation.4 | async-start | bytes 4194304 | tf_op jit(solution)/shard_map/all_to_all | solution.py:914
  237.5 29.8 %all-to-all-start.5 = ((bf16[8,128,512]{2,1,0:T(8,128)(2,1)}), bf16[8,128,512]{2,1,0:T(8,128)(2,1)}, u32[]{:S(2)}, u32[]{:S(2)}) async-start(bf16[8,128,512]{2,1,0:T(8,128)(2,1)} %get-tuple-element.111), calls=%async_computation.5 | async-start | bytes 2097152 | tf_op jit(solution)/shard_map/all_to_all | solution.py:914
  276.6 20.2 %all-to-all-start.8 = ((bf16[8,128,512]{2,1,0:T(8,128)(2,1)}), bf16[8,128,512]{2,1,0:T(8,128)(2,1)}, u32[]{:S(2)}, u32[]{:S(2)}) async-start(bf16[8,128,512]{2,1,0:T(8,128)(2,1)} %get-tuple-element.118), calls=%async_computation.8 | async-start | bytes 2097152 | tf_op jit(solution)/shard_map/all_to_all | solution.py:914
  296.7 47.4 %all-to-all-start.7 = ((bf16[8,256,512]{2,1,0:T(8,128)(2,1)}), bf16[8,256,512]{2,1,0:T(8,128)(2,1)}, u32[]{:S(2)}, u32[]{:S(2)}) async-start(bf16[8,256,512]{2,1,0:T(8,128)(2,1)} %bitcast.38), calls=%async_computation.7 | async-start | bytes 4194304 | tf_op jit(solution)/shard_map/all_to_all | solution.py:914
  301.1 181.5 %reduce-scatter.2.cloned.1.call-start = ((), (), s32[]{:S(2)}) async-start(), calls=%async_computation.14 | async-start | bytes 5242880 | tf_op jit(solution)/shard_map/reduce_scatter | solution.py:1099
  422.3 24.7 %all-to-all-start.11 = ((bf16[8,4,16,1536]{3,2,1,0:T(8,128)(2,1)}), bf16[8,4,16,1536]{3,2,1,0:T(8,128)(2,1)S(1)}, u32[]{:S(2)}, u32[]{:S(2)}) async-start(bf16[8,4,16,1536]{3,2,1,0:T(8,128)(2,1)} %get-tuple-element.139), calls=%async_computation.11 | async-start | bytes 3145728 | tf_op jit(solution)/shard_map/all_to_all | solution.py:914
  446.9 15.0 %all-to-all-start.10 = ((bf16[4,4,16,1792]{3,2,1,0:T(8,128)(2,1)}), bf16[4,4,16,1792]{3,2,1,0:T(8,128)(2,1)S(1)}, u32[]{:S(2)}, u32[]{:S(2)}) async-start(bf16[4,4,16,1792]{3,2,1,0:T(8,128)(2,1)} %fusion), calls=%async_computation.10 | async-start | bytes 1835008 | tf_op jit(solution)/shard_map/all_to_all | solution.py:1180
  462.9 17.1 %all-to-all-start.12 = ((bf16[4,16,3328]{2,1,0:T(8,128)(2,1)}), bf16[4,16,3328]{2,1,0:T(8,128)(2,1)S(1)}, u32[]{:S(2)}, u32[]{:S(2)}) async-start(bf16[4,16,3328]{2,1,0:T(8,128)(2,1)} %pad_maximum_fusion.2), calls=%async_computation.12 | async-start | bytes 851968 | tf_op jit(solution)/shard_map/all_to_all | solution.py:1202
  (20 other events, 213.2 us)
Sparse Core Ops, SparseCore 0:
  28.0 80.2 all-gather.2
  344.3 79.8 reduce-scatter.1
where the time goes:
time: 501 us; the launch traced here: 492 us
  Pallas kernels  231 us (46%)
  waiting for transfers between devices  125 us (25%)
  starting transfers between devices  61.6 us (12%)
  blocking collectives  40 us (8%)
  between operations  14.6 us (3%)
  local copies, waits for them, and re-layouts  12.3 us (2%)
  other arithmetic  7.51 us (1%)
    all_to_all x9, waiting for transfers between devices, exchange(): lax.all_to_all(values, 'fsdp', split_axis=0, concat_axis=0, tiled=True)  87.6 us
    pallas_call x2, Pallas kernels, on_device(): pl.pallas_call(partial(expert_kernel, groups), grid=(half_slots // step_r...  52.8 us
    pallas_call x5, Pallas kernels, call(): pl.pallas_call(kernel, out_shape=outs, in_specs=in_vmem(len(inputs)), out...  46 us
    all_to_all x2, blocking collectives, exchange(): lax.all_to_all(values, 'fsdp', split_axis=0, concat_axis=0, tiled=True)  40 us
    all_to_all x9, starting transfers between devices, exchange(): lax.all_to_all(values, 'fsdp', split_axis=0, concat_axis=0, tiled=True)  38.9 us
    pallas_call x2, Pallas kernels, on_device(): pl.pallas_call(partial(data_back_kernel, experts, groups, h), grid=(exper...  31.6 us
    pallas_call x1, Pallas kernels, on_device(): pl.pallas_call(partial(weight_back_kernel, groups, steps, joined), name='...  27.2 us
    pallas_call x1, Pallas kernels, on_device(): pl.pallas_call(partial(attend_kernel, experts, shape), name='attend', out...  26.8 us
  transfers between devices with their start and end apart: 26, of which 14 were waited for; matrix products, arithmetic and copies ran while one was open for 2% of the time, Pallas kernels for 42%

commit v1 on v0

--- a/solution.py
+++ b/solution.py
@@ -88,9 +88,8 @@
     return high, (values - high.astype(F32)).astype(BF)
 
 
-def ranks_kernel(capacity, meta_ref, pair_ref, rank_ref, rank_t_ref, place_ref, scal_ref):
+def ranks_kernel(meta_ref, rank_ref, rank_t_ref):
     tok = meta_ref.shape[0]
-    size = capacity // HALVES
     tri = lax.broadcasted_iota(jnp.int32, (BLOCK, BLOCK), 0) >= lax.broadcasted_iota(
         jnp.int32, (BLOCK, BLOCK), 1
     )
@@ -100,27 +99,27 @@
     def block(b, carry):
         rows = pl.ds(b * BLOCK, BLOCK)
         meta = meta_ref[rows, :]
-        pair = pair_ref[rows, :]
-        scal_ref[rows, :] = jnp.where(lane == 0, pair[:, 0:1], pair[:, 1:2])
         pick = ((lane == meta[:, 4:5]) | (lane == meta[:, 5:6])) & (meta[:, 6:7] >= STEP)
-        ones = jnp.where(pick, 1.0, 0.0)
-        count = dot(tri, ones.astype(BF)) + carry
-        rank = jnp.where(pick, count - 1.0, -1.0)
-        rank_ref[rows, :] = rank
-        place = jnp.full((BLOCK, LANES), -1, jnp.int32)
-        for k in range(F_TOP):
-            route = meta[:, 4 + k : 5 + k]
-            mine = jnp.sum(jnp.where(lane == route, rank, 0.0), axis=1, keepdims=True)
-            mine = mine.astype(jnp.int32)
-            for h in range(HALVES):
-                within = mine - h * size
-                dest = jnp.where((within >= 0) & (within < size), route * size + within, -1)
-                place = jnp.where(lane == F_TOP * h + k, dest, place)
-        place_ref[rows, :] = place
+        count = dot(tri, jnp.where(pick, 1.0, 0.0).astype(BF)) + carry
+        rank_ref[rows, :] = jnp.where(pick, count - 1.0, -1.0)
         return count[BLOCK - 1 :, :]
 
     lax.fori_loop(0, tok // BLOCK, block, jnp.zeros((1, LANES), F32))
     rank_t_ref[...] = jnp.transpose(rank_ref[...])[: rank_t_ref.shape[0], :].astype(jnp.int32)
+
+
+def slot_places(capacity, meta, rank, lane):
+    size = capacity // HALVES
+    place = jnp.full(rank.shape, -1, jnp.int32)
+    for k in range(F_TOP):
+        route = meta[:, 4 + k : 5 + k]
+        mine = jnp.sum(jnp.where(lane == route, rank, 0.0), axis=1, keepdims=True)
+        mine = mine.astype(jnp.int32)
+        for h in range(HALVES):
+            within = mine - h * size
+            dest = jnp.where((within >= 0) & (within < size), route * size + within, -1)
+            place = jnp.where(lane == F_TOP * h + k, dest, place)
+    return place
 
 
 def gather_pair(rank_t_ref, rows_ref, starts, slots_refs, pair):
@@ -384,15 +383,19 @@
 
 def combine_first_kernel(
     experts,
+    capacity,
     back_ref,
-    place_ref,
+    rank_ref,
     tail_ref,
     meta_ref,
     fgate_ref,
     cot_ref,
+    pair_ref,
     branch_ref,
     cols_ref,
     live_ref,
+    place_ref,
+    scal_ref,
     dense_ref,
 ):
     halt_row = vector_row(turned_tail(tail_ref[...]), A_EXP + experts, 4)
@@ -402,9 +405,13 @@
         rows = pl.ds(b * BLOCK, BLOCK)
         meta = meta_ref[rows, :]
         fgate = fgate_ref[rows, :]
+        pair = pair_ref[rows, :]
+        scal_ref[rows, :] = jnp.where(lane == 0, pair[:, 0:1], pair[:, 1:2])
+        place = slot_places(capacity, meta, rank_ref[rows, :], lane)
+        place_ref[rows, :] = place
         branch, cols = combine_sums(
             0,
-            place_ref[rows, :],
+            place,
             back_ref,
             fgate,
             cot_ref[rows, :].astype(F32),
@@ -679,20 +686,26 @@
 
 def input_back_kernel(
     experts,
-    tok_ref,
-    w_ref,
-    meta_ref,
-    gh_ref,
+    tok_hbm,
+    w_hbm,
+    meta_hbm,
+    gh_hbm,
+    gla_hbm,
     gslot_ref,
-    gla_ref,
     rvin_ref,
     vecin_ref,
     halt_ref,
     lse_ref,
     slotq_ref,
     kv_ref,
+    gin_hbm,
+    pack_ref,
+    tok_ref,
+    w_ref,
+    meta_ref,
+    gh_ref,
+    gla_ref,
     gin_ref,
-    pack_ref,
     gx_ref,
     wide_ref,
     acc_ref,
@@ -702,13 +715,26 @@
     vx_ref,
     lset_ref,
     gq_ref,
+    load_sems,
+    store_sems,
 ):
+    loads = [
+        pltpu.make_async_copy(source, target, load_sems.at[i])
+        for i, (source, target) in enumerate(
+            (
+                (tok_hbm, tok_ref),
+                (w_hbm, w_ref),
+                (meta_hbm, meta_ref),
+                (gh_hbm, gh_ref),
+                (gla_hbm, gla_ref),
+            )
+        )
+    ]
+    for load in loads:
+        load.start()
     tok = tok_ref.shape[0]
     blocks = tok // BLOCK
     first = A_EXP + experts
-    rows_t = transposed_tail(w_ref)
-    low_t = rows_t.astype(BF)
-    gain_one, shift_one = (vector_row(rows_t, first, i) for i in range(2))
     lane = lane_ids(BLOCK)
     upper = lane >= HEAD
     lane_half = jnp.where(upper, 1, 0)
@@ -756,6 +782,16 @@
 
         lax.fori_loop(0, A_TOP // 2, pair, 0)
 
+    for load in loads:
+        load.wait()
+    rows_t = transposed_tail(w_ref)
+    low_t = rows_t.astype(BF)
+    gain_one, shift_one = (vector_row(rows_t, first, i) for i in range(2))
+
+    def stored(b):
+        rows = pl.ds(b * BLOCK, BLOCK)
+        return pltpu.make_async_copy(gin_ref.at[rows], gin_hbm.at[rows], store_sems.at[b])
+
     def input_back(b, gkv_sum):
         rows = pl.ds(b * BLOCK, BLOCK)
         meta = meta_ref[rows, :]
@@ -779,6 +815,7 @@
         vec_ref[0:1, :] += jnp.sum(grad * hat, axis=0, keepdims=True)
         vec_ref[1:2, :] += jnp.sum(grad, axis=0, keepdims=True)
         gin_ref[rows, :] = (gh_ref[rows, :] + norm_back(grad, hat, inv, gain_one)).astype(BF)
+        stored(b).start()
         return gkv_sum + dot(normed, gkv, TN)
 
     gkv_sum = lax.fori_loop(0, blocks, input_back, jnp.zeros((D, LANES), F32))
@@ -787,6 +824,8 @@
     turned = pltpu.roll(jnp.transpose(vec_ref[...]), first, 1)
     tail = jnp.where(lane_ids(D) < first, rv_ref[...], turned)
     store_grads(pack_ref, tail.astype(BF), WIDTH + LANES)
+    for b in range(blocks):
+        stored(b).wait()
 
 
 VMEM_LIMIT = 60 * 1024 * 1024
@@ -891,15 +930,8 @@
     half = capacity // HALVES
     half_slots = slots // HALVES
 
-    rank, rank_t, place, scal = call(
-        partial(ranks_kernel, capacity),
-        (meta, scal),
-        (
-            whole((tok, LANES), F32),
-            whole((experts, tok), jnp.int32),
-            whole((tok, LANES), jnp.int32),
-            whole((tok, LANES), F32),
-        ),
+    rank, rank_t = call(
+        ranks_kernel, (meta,), (whole((tok, LANES), F32), whole((experts, tok), jnp.int32))
     )
 
     def gather_rows(rows, name, starts):
@@ -982,20 +1014,22 @@
 
     tail_spec = pl.BlockSpec((D, LANES), lambda s: (0, RV_AT // LANES))
     full = pl.BlockSpec(memory_space=pltpu.VMEM)
-    sums = pl.pallas_call(
-        partial(combine_first_kernel, experts),
+    *sums, place, scal = pl.pallas_call(
+        partial(combine_first_kernel, experts, capacity),
         name="combine_first",
         grid=(1,),
         out_shape=(
             whole((tok, D), F32),
             whole((tok, LANES), F32),
             whole((3, max(16, experts), tok), BF),
+            whole((tok, LANES), jnp.int32),
+            whole((tok, LANES), F32),
         ),
-        in_specs=[full, full, tail_spec, full, full, full],
-        out_specs=[full] * 3,
+        in_specs=[full, full, tail_spec, full, full, full, full],
+        out_specs=[full] * 5,
         scratch_shapes=[pltpu.VMEM((tok, LANES), F32)],
         compiler_params=params,
-    )(back[0], place, weights, meta, fgate, cot_out)
+    )(back[0], rank, weights, meta, fgate, cot_out, scal)
     back[1], cot_second = lax.optimization_barrier((back[1], cot_slots[1]))
     owned_cot.append(exchange(cot_second))
 
@@ -1182,11 +1216,20 @@
         )
         return jnp.sum(came.astype(F32), axis=0).astype(BF)
 
-    grad_in, grads = call(
+    anywhere = pl.BlockSpec(memory_space=pl.ANY)
+    grad_in, grads = pl.pallas_call(
         partial(input_back_kernel, experts),
-        (tokens, weights, meta, gh, gslot, gla, rv, vec, halt_grad, logs, slotq, kv),
-        (whole((tok, D), BF), last_shape),
-        (
+        name="input_back",
+        out_shape=(whole((tok, D), BF), last_shape),
+        in_specs=[anywhere] * 5 + [full] * 7,
+        out_specs=[anywhere, full],
+        scratch_shapes=[
+            pltpu.VMEM((tok, D), BF),
+            pltpu.VMEM((D, PACK), BF),
+            pltpu.VMEM(meta.shape, jnp.int32),
+            pltpu.VMEM((tok, D), F32),
+            pltpu.VMEM((tok, LANES), F32),
+            pltpu.VMEM((tok, D), BF),
             pltpu.VMEM((2, 2, tok, LANES), F32),
             pltpu.VMEM((BLOCK, WIDTH), BF),
             pltpu.VMEM((D, WIDTH), F32),
@@ -1196,8 +1239,11 @@
             pltpu.VMEM((2, tok, LANES), BF),
             pltpu.VMEM((LANES, tok), F32),
             pltpu.VMEM((2, tok, LANES), F32),
-        ),
-    )
+            pltpu.SemaphoreType.DMA((5,)),
+            pltpu.SemaphoreType.DMA((tok // BLOCK,)),
+        ],
+        compiler_params=pltpu.CompilerParams(vmem_limit_bytes=VMEM_LIMIT),
+    )(tokens, weights, meta, gh, gla, gslot, rv, vec, halt_grad, logs, slotq, kv)
     part = jnp.concatenate([reduced_last(grads), part_out], axis=2)
     came = lax.all_to_all(part, "dp", split_axis=0, concat_axis=0, tiled=True)
     total = jnp.sum(came.astype(F32), axis=0)

time: 501 us -> 500 us (level)
    pallas_call x5 -> x4, Pallas kernels: 46 us -> 19.6 us  [call(): pl.pallas_call(kernel, out_shape=outs, in_specs=in_vmem(len(inputs)), out...]
    pallas_call x1 -> x2, Pallas kernels: 9.85 us -> 34.9 us  [the longest x1 22.5 us: on_device(): pl.pallas_call(partial(input_back_kernel, experts), name='input_back', ou...]
  transfers between devices with their start and end apart: 26 -> 26, of which waited for: 14 -> 14; matrix products, arithmetic and copies ran while one was open for 2% -> 2% of each run, Pallas kernels for 42% -> 41%
where the time goes in v1:
time: 500 us; the launch traced here: 491 us
  Pallas kernels  230 us (46%)
  waiting for transfers between devices  125 us (25%)
  starting transfers between devices  61.8 us (12%)
  blocking collectives  40 us (8%)
  between operations  14.7 us (3%)
  local copies, waits for them, and re-layouts  11.8 us (2%)
  other arithmetic  7.49 us (1%)
    all_to_all x9, waiting for transfers between devices, exchange(): lax.all_to_all(values, 'fsdp', split_axis=0, concat_axis=0, tiled=True)  87.6 us
    pallas_call x2, Pallas kernels, on_device(): pl.pallas_call(partial(expert_kernel, groups), grid=(half_slots // step_r...  52.8 us
    all_to_all x2, blocking collectives, exchange(): lax.all_to_all(values, 'fsdp', split_axis=0, concat_axis=0, tiled=True)  40 us
    all_to_all x9, starting transfers between devices, exchange(): lax.all_to_all(values, 'fsdp', split_axis=0, concat_axis=0, tiled=True)  39 us
    pallas_call x2, Pallas kernels, on_device(): pl.pallas_call(partial(data_back_kernel, experts, groups, h), grid=(exper...  31.6 us
    pallas_call x1, Pallas kernels, on_device(): pl.pallas_call(partial(weight_back_kernel, groups, steps, joined), name='...  27.2 us
    pallas_call x1, Pallas kernels, on_device(): pl.pallas_call(partial(attend_kernel, experts, shape), name='attend', out...  26.7 us
    pallas_call x1, Pallas kernels, on_device(): pl.pallas_call(partial(input_back_kernel, experts), name='input_back', ou...  22.5 us
  transfers between devices with their start and end apart: 26, of which 14 were waited for; matrix products, arithmetic and copies ran while one was open for 2% of the time, Pallas kernels for 41%

profile of v1, /device:TPU:0, one launch (start us, length us, event | category | flops | bytes accessed | tf_op | source)
XLA Modules:
  0.0 490.9 jit_solution(11452435537324371893)
XLA Ops:
  15.8 4.9 collective-permute-done.1
  28.0 5.3 %collective-permute-done.6.refs_7_ = bf16[4,16,3328]{2,1,0:T(8,128)(2,1)S(1)} collective-permute-done((bf16[4,16,3328]{2,1,0:T(8,128)(2,1)S(1)}, bf16[4,16,3328]{2,1,0:T(8,128)(2,1)S(1)}, u32[]{:S(2)}, u32[]{:S(2)}) %collective-permute-start.6) | collective-permute-done | bytes 426016 | tf_op jit(solution)/shard_map/ppermute | solution.py:872
  45.4 5.4 %shard_map.214 = bf16[8,256,512]{2,1,0:T(8,128)(2,1)} custom-call(s32[8,1024]{1,0:T(8,128)} %get-tuple-element.78.rank_t_ref.refs_2_, bf16[1024,512]{1,0:T(8,128)(2,1)} %cot_ref.5), custom_call_target="tpu_custom_call" | custom-call | tf_op jit(solution)/shard_map/pallas_call | solution.py:844
  56.4 26.7 %attend.1 = (bf16[512,3328]{1,0:T(8,128)(2,1)}, bf16[2,1024,128]{2,1,0:T(8,128)(2,1)}, bf16[1024,128]{1,0:T(8,128)(2,1)}, f32[2,1024,128]{2,1,0:T(8,128)}, f32[1...) custom-call(bf16[1024,512]{1,0:T(8,128)(2,1)} %tok_hbm.1, ...), custom_call_target="tpu_custom_call" | custom-call | tf_op jit(solution)/shard_map/attend/pallas_call | solution.py:965
  87.5 5.4 %shard_map.215 = bf16[8,256,512]{2,1,0:T(8,128)(2,1)} custom-call(s32[8,1024]{1,0:T(8,128)} %get-tuple-element.78.rank_t_ref.refs_2_, bf16[1024,512]{1,0:T(8,128)(2,1)} %get-tuple-element.89.rows_ref), custom_call_target="tpu_custom_call" | custom-call | tf_op jit(solution)/shard_map/pallas_call | solution.py:844
  92.9 21.2 %all-to-all-done.1 = bf16[8,256,512]{2,1,0:T(8,128)(2,1)} async-done(((bf16[8,256,512]{2,1,0:T(8,128)(2,1)}), bf16[8,256,512]{2,1,0:T(8,128)(2,1)}, u32[]{:S(2)}, u32[]{:S(2)}) %all-to-all-start.1) | async-done | bytes 2097184 | tf_op jit(solution)/shard_map/all_to_all | solution.py:946
  119.0 26.6 %all-to-all-done.2 = bf16[8,256,512]{2,1,0:T(8,128)(2,1)} async-done(((bf16[8,256,512]{2,1,0:T(8,128)(2,1)}), bf16[8,256,512]{2,1,0:T(8,128)(2,1)}, u32[]{:S(2)}, u32[]{:S(2)}) %all-to-all-start.2) | async-done | bytes 2097184 | tf_op jit(solution)/shard_map/all_to_all | solution.py:946
  145.6 26.5 %shard_map.216 = (bf16[2048,512]{1,0:T(8,128)(2,1)}, bf16[4,2048,512]{2,1,0:T(8,128)(2,1)}, bf16[4,2048,512]{2,1,0:T(8,128)(2,1)}) custom-call(bf16[2048,512]{1,0:T(8,128)(2,1)} %bitcast.8.x_ref.refs_4_, bf16[4,1024,512]{2,1,0:T(8,128)(2,1)} %bitcast.30, bf16[4,1024,512]{2,1,0:T(8,128)(2,1)} %bitcast.31), custom_call_target="tpu_custom_call" | custom-call | tf_op jit(solution)/shard_map/pallas_call | solution.py:999
  176.4 26.3 %shard_map.218 = (bf16[2048,512]{1,0:T(8,128)(2,1)}, bf16[4,2048,512]{2,1,0:T(8,128)(2,1)}, bf16[4,2048,512]{2,1,0:T(8,128)(2,1)}) custom-call(bf16[2048,512]{1,0:T(8,128)(2,1)} %bitcast.7.x_ref.refs_0_, bf16[4,1024,512]{2,1,0:T(8,128)(2,1)} %bitcast.32, bf16[4,1024,512]{2,1,0:T(8,128)(2,1)} %bitcast.33), custom_call_target="tpu_custom_call" | custom-call | tf_op jit(solution)/shard_map/pallas_call | solution.py:999
  207.4 5.4 %shard_map.217 = (bf16[8,128,512]{2,1,0:T(8,128)(2,1)}, bf16[8,128,512]{2,1,0:T(8,128)(2,1)}) custom-call(s32[8,1024]{1,0:T(8,128)} %get-tuple-element.78.rank_t_ref.refs_2_, bf16[1024,512]{1,0:T(8,128)(2,1)} %cot_ref.5), custom_call_target="tpu_custom_call" | custom-call | tf_op jit(solution)/shard_map/pallas_call | solution.py:844
  212.7 21.3 %all-to-all-done.4 = bf16[8,256,512]{2,1,0:T(8,128)(2,1)} async-done(((bf16[8,256,512]{2,1,0:T(8,128)(2,1)}), bf16[8,256,512]{2,1,0:T(8,128)(2,1)}, u32[]{:S(2)}, u32[]{:S(2)}) %all-to-all-start.4) | async-done | bytes 2097184 | tf_op jit(solution)/shard_map/all_to_all | solution.py:946
  239.3 12.4 %combine_first.1 = (f32[1024,512]{1,0:T(8,128)}, f32[1024,128]{1,0:T(8,128)}, bf16[3,16,1024]{2,1,0:T(8,128)(2,1)}, s32[1024,128]{1,0:T(8,128)}, f32[1024,128]{1,0:T(8,128)}) custom-call(bf16[2048,512]{1,0:T(8,128)(2,1)} %bitcast.15.back_ref, f32[1024,128]{1,0:T(8,128)} %get-tuple-element.99.rank_ref, ...), custom_call_target="tpu_custom_call" | custom-call | tf_op jit(solution)/shard_map/combine_first/pallas_call | solution.py:1017
  251.8 15.7 %combine.1 = (bf16[1024,512]{1,0:T(8,128)(2,1)}, f32[1024,128]{1,0:T(8,128)}, f32[1024,128]{1,0:T(8,128)}, f32[1024,128]{1,0:T(8,128)}, f32[8,512]{1,0:T(8,128)}, /*index=5*/bf16[8,8,512]{2,1,0:T(8,128)(2,1)}) custom-call(bf16[2048,512]{1,0:T(8,128)(2,1)} %bitcast.13.back_ref, f32[1024,512]{1,0:T(8,128)} %get-tuple-element.102.branch_ref, ...), custom_call_target="tpu_custom_call" | custom-call | tf_op jit(solution)/shard_map/combine/pallas_call | solution.py:1039
  267.5 9.2 %all_to_all.65.refs_1_.refs_2_ = bf16[8,8,512]{2,1,0:T(8,128)(2,1)} all-to-all(bf16[8,8,512]{2,1,0:T(8,128)(2,1)} %get-tuple-element.113), channel_id=1, replica_groups=mesh['dp'=4,'fsdp'=8] {'fsdp'}, dimensions={0} | all-to-all | bytes 131072 | tf_op jit(solution)/shard_map/all_to_all | solution.py:946
  281.1 15.8 %shard_map.219 = (bf16[4,2048,512]{2,1,0:T(8,128)(2,1)}, bf16[2048,512]{1,0:T(8,128)(2,1)}, bf16[2048,512]{1,0:T(8,128)(2,1)}) custom-call(bf16[2048,512]{1,0:T(8,128)(2,1)} %bitcast.18.refs_0_, bf16[8,8,512]{2,1,0:T(8,128)(2,1)} %all_to_all.65.refs_1_.refs_2_, bf16[512,3328]{1,0:T(8,128)(2,1)} %get-tuple-element.100.tail_ref.refs_2_.refs_3_.w_ref.w_hbm, ...), custom_call_target="tpu_custom_call" | custom-call | tf_op jit(solution)/shard_map/pallas_call | solution.py:1081
  301.3 15.8 %shard_map.220 = (bf16[4,2048,512]{2,1,0:T(8,128)(2,1)}, bf16[2048,512]{1,0:T(8,128)(2,1)}, bf16[2048,512]{1,0:T(8,128)(2,1)}) custom-call(bf16[1024,512]{1,0:T(8,128)(2,1)} %bitcast.20.refs_0_, bf16[1024,512]{1,0:T(8,128)(2,1)} %bitcast.21.refs_1_, bf16[8,8,512]{2,1,0:T(8,128)(2,1)} %all_to_all.65.refs_1_.refs_2_, ...), custom_call_target="tpu_custom_call" | custom-call | tf_op jit(solution)/shard_map/pallas_call | solution.py:1081
  317.1 27.2 %weight_back.1 = bf16[4,1024,512]{2,1,0:T(8,128)(2,1)} custom-call(bf16[2048,512]{1,0:T(8,128)(2,1)} %bitcast.7.x_ref.refs_0_, bf16[2048,512]{1,0:T(8,128)(2,1)} %get-tuple-element.140.refs_1_, bf16[4,2048,512]{2,1,0:T(8,128)(2,1)} %get-tuple-element.141.refs_2_, bf16[4,2048,512]{2,1,0:T(8,128)(2,1)} %get-tuple-element.142.refs_3_, ...), custom_call_target="tpu_custom_call" | custom-call | tf_op jit(solution)/shard_map/weight_back/pallas_call | solution.py:1122
  345.9 30.8 %all_to_all.66.second_ref = bf16[8,256,512]{2,1,0:T(8,128)(2,1)} all-to-all(bf16[8,256,512]{2,1,0:T(8,128)(2,1)S(1)} %bitcast.39), channel_id=1, replica_groups=mesh['dp'=4,'fsdp'=8] {'fsdp'}, dimensions={0} | all-to-all | bytes 4194304 | tf_op jit(solution)/shard_map/all_to_all | solution.py:946
  376.7 21.3 %hidden_back.1 = (bf16[8,4,16,1536]{3,2,1,0:T(8,128)(2,1)}, f32[1024,512]{1,0:T(8,128)}, bf16[2,1024,128]{2,1,0:T(8,128)(2,1)}, f32[1024,128]{1,0:T(8,128)}, f32...) custom-call(bf16[8,256,512]{2,1,0:T(8,128)(2,1)} %all-to-all-done.7.first_ref, ...), custom_call_target="tpu_custom_call" | custom-call | tf_op jit(solution)/shard_map/hidden_back/pallas_call | solution.py:1149
  398.0 22.5 %input_back.1 = (bf16[1024,512]{1,0:T(8,128)(2,1)}, bf16[2,4,4,16,1792]{4,3,2,1,0:T(8,128)(2,1)}) custom-call(bf16[1024,512]{1,0:T(8,128)(2,1)} %tok_hbm.1, bf16[512,3328]{1,0:T(8,128)(2,1)} %get-tuple-element.100.tail_ref.refs_2_.refs_3_.w_ref.w_hbm, s32[1024,8]{1,0:T(8,128)} %copy.54.meta_ref.refs_1_.meta_hbm, f32[1024,512]{1,0:T(8,128)} %get-tuple-element.128.gh_hbm, ...), custom_call_target="tpu_custom_call" | custom-call | tf_op jit(solution)/shard_map/input_back/pallas_call | solution.py:1220
  427.0 18.2 %all-to-all-done.11 = bf16[8,4,16,1536]{3,2,1,0:T(8,128)(2,1)S(1)} async-done(((bf16[8,4,16,1536]{3,2,1,0:T(8,128)(2,1)}), bf16[8,4,16,1536]{3,2,1,0:T(8,128)(2,1)S(1)}, u32[]{:S(2)}, u32[]{:S(2)}) %all-to-all-start.11) | async-done | bytes 1572896 | tf_op jit(solution)/shard_map/all_to_all | solution.py:946
  449.0 11.2 %all-to-all-done.10 = bf16[4,4,16,1792]{3,2,1,0:T(8,128)(2,1)S(1)} async-done(((bf16[4,4,16,1792]{3,2,1,0:T(8,128)(2,1)}), bf16[4,4,16,1792]{3,2,1,0:T(8,128)(2,1)S(1)}, u32[]{:S(2)}, u32[]{:S(2)}) %all-to-all-start.10) | async-done | bytes 917536 | tf_op jit(solution)/shard_map/all_to_all | solution.py:1214
  461.2 6.3 %all-to-all-start.12 = ((bf16[4,16,3328]{2,1,0:T(8,128)(2,1)}), bf16[4,16,3328]{2,1,0:T(8,128)(2,1)S(1)}, u32[]{:S(2)}, u32[]{:S(2)}) async-start(bf16[4,16,3328]{2,1,0:T(8,128)(2,1)} %pad_maximum_fusion.2), calls=%async_computation.12 | async-start | bytes 851968 | tf_op jit(solution)/shard_map/all_to_all | solution.py:1248
  468.2 10.1 %all-to-all-done.12 = bf16[4,16,3328]{2,1,0:T(8,128)(2,1)S(1)} async-done(((bf16[4,16,3328]{2,1,0:T(8,128)(2,1)}), bf16[4,16,3328]{2,1,0:T(8,128)(2,1)S(1)}, u32[]{:S(2)}, u32[]{:S(2)}) %all-to-all-start.12) | async-done | bytes 426016 | tf_op jit(solution)/shard_map/all_to_all | solution.py:1248
  (105 shorter events, 84.7 us)
Async XLA Ops:
  7.2 111.8 %all-gather.3.cloned.1.call-start = ((), (), s32[]{:S(2)}) async-start(), calls=%async_computation.15 | async-start | bytes 5242880 | tf_op jit(solution)/shard_map/all_gather | solution.py:923
  9.6 11.1 %collective-permute-start.1 = (bf16[16,3328]{1,0:T(8,128)(2,1)S(1)}, bf16[16,3328]{1,0:T(8,128)(2,1)S(1)}, u32[]{:S(2)}, u32[]{:S(2)}) collective-permute-start(bf16[16,3328]{1,0:T(8,128)(2,1)S(1)} %get-tuple-element.191), channel_id=1, source_target_pairs={{16,0},{24,8},{0,16},{8,24},{17,1},{25,9},{1,17},{9,25},{18,2},{26... | collective-permute-start | bytes 319496 | tf_op jit(solution)/shard_map/ppermute | solution.py:868
  13.7 6.9 %collective-permute-start = (bf16[16,3328]{1,0:T(8,128)(2,1)S(1)}, bf16[16,3328]{1,0:T(8,128)(2,1)S(1)}, u32[]{:S(2)}, u32[]{:S(2)}) collective-permute-start(bf16[16,3328]{1,0:T(8,128)(2,1)S(1)} %get-tuple-element.191), channel_id=1, source_target_pairs={{8,0},{16,8},{24,16},{0,24},{9,1},{17,9},{25,17},{1,25},{10,2},{18... | collective-permute-start | bytes 319496 | tf_op jit(solution)/shard_map/ppermute | solution.py:868
  15.1 7.3 %collective-permute-start.2 = (bf16[16,3328]{1,0:T(8,128)(2,1)S(1)}, bf16[16,3328]{1,0:T(8,128)(2,1)S(1)}, u32[]{:S(2)}, u32[]{:S(2)}) collective-permute-start(bf16[16,3328]{1,0:T(8,128)(2,1)S(1)} %get-tuple-element.191), channel_id=1, source_target_pairs={{24,0},{0,8},{8,16},{16,24},{25,1},{1,9},{9,17},{17,25},{26,2},{2,... | collective-permute-start | bytes 319496 | tf_op jit(solution)/shard_map/ppermute | solution.py:868
  22.5 10.8 %collective-permute-start.6 = (bf16[4,16,3328]{2,1,0:T(8,128)(2,1)S(1)}, bf16[4,16,3328]{2,1,0:T(8,128)(2,1)S(1)}, u32[]{:S(2)}, u32[]{:S(2)}) collective-permute-start(bf16[4,16,3328]{2,1,0:T(8,128)(2,1)S(1)} %pad_maximum_fusion.1.refs_3_), channel_id=1, source_target_pairs={{0,4},{1,5},{2,6},{3,7},{4,0},{5,1},{6,2},{7,3},{8,12},{9,13},{10,... | collective-permute-start | bytes 1277960 | tf_op jit(solution)/shard_map/ppermute | solution.py:872
  24.1 10.8 %collective-permute-start.4 = (bf16[4,16,3328]{2,1,0:T(8,128)(2,1)S(1)}, bf16[4,16,3328]{2,1,0:T(8,128)(2,1)S(1)}, u32[]{:S(2)}, u32[]{:S(2)}) collective-permute-start(bf16[4,16,3328]{2,1,0:T(8,128)(2,1)S(1)} %pad_maximum_fusion.1.refs_3_), channel_id=1, source_target_pairs={{0,2},{1,3},{2,0},{3,1},{4,6},{5,7},{6,4},{7,5},{8,10},{9,11},{10,... | collective-permute-start | bytes 1277960 | tf_op jit(solution)/shard_map/ppermute | solution.py:872
  27.9 22.9 %collective-permute-start.3 = (bf16[4,16,3328]{2,1,0:T(8,128)(2,1)S(1)}, bf16[4,16,3328]{2,1,0:T(8,128)(2,1)S(1)}, u32[]{:S(2)}, u32[]{:S(2)}) collective-permute-start(bf16[4,16,3328]{2,1,0:T(8,128)(2,1)S(1)} %pad_maximum_fusion.1.refs_3_), channel_id=1, source_target_pairs={{0,1},{1,0},{2,3},{3,2},{4,5},{5,4},{6,7},{7,6},{8,9},{9,8},{10,11... | collective-permute-start | bytes 1277960 | tf_op jit(solution)/shard_map/ppermute | solution.py:872
  33.3 5.9 %collective-permute-start.9 = (bf16[2,16,3328]{2,1,0:T(8,128)(2,1)S(1)}, bf16[2,16,3328]{2,1,0:T(8,128)(2,1)S(1)}, u32[]{:S(2)}, u32[]{:S(2)}) collective-permute-start(bf16[2,16,3328]{2,1,0:T(8,128)(2,1)S(1)} %slice.49), channel_id=1, source_target_pairs={{0,2},{1,3},{2,0},{3,1},{4,6},{5,7},{6,4},{7,5},{8,10},{9,11},{10,... | collective-permute-start | bytes 638984 | tf_op jit(solution)/shard_map/ppermute | solution.py:872
  36.5 14.4 %collective-permute-start.7 = (bf16[4,16,3328]{2,1,0:T(8,128)(2,1)S(1)}, bf16[4,16,3328]{2,1,0:T(8,128)(2,1)S(1)}, u32[]{:S(2)}, u32[]{:S(2)}) collective-permute-start(bf16[4,16,3328]{2,1,0:T(8,128)(2,1)S(1)} %collective-permute-done.6.refs_7_), channel_id=1, source_target_pairs={{0,1},{1,0},{2,3},{3,2},{4,5},{5,4},{6,7},{7,6},{8,9},{9,8},{10,11... | collective-permute-start | bytes 1277960 | tf_op jit(solution)/shard_map/ppermute | solution.py:872
  36.5 14.4 %collective-permute-start.5 = (bf16[4,16,3328]{2,1,0:T(8,128)(2,1)S(1)}, bf16[4,16,3328]{2,1,0:T(8,128)(2,1)S(1)}, u32[]{:S(2)}, u32[]{:S(2)}) collective-permute-start(bf16[4,16,3328]{2,1,0:T(8,128)(2,1)S(1)} %collective-permute-done.4.refs_5_), channel_id=1, source_target_pairs={{0,1},{1,0},{2,3},{3,2},{4,5},{5,4},{6,7},{7,6},{8,9},{9,8},{10,11... | collective-permute-start | bytes 1277960 | tf_op jit(solution)/shard_map/ppermute | solution.py:872
  39.2 11.6 %collective-permute-start.11 = (bf16[2,16,3328]{2,1,0:T(8,128)(2,1)S(1)}, bf16[2,16,3328]{2,1,0:T(8,128)(2,1)S(1)}, u32[]{:S(2)}, u32[]{:S(2)}) collective-permute-start(bf16[2,16,3328]{2,1,0:T(8,128)(2,1)S(1)} %collective-permute-done.9.refs_10_), channel_id=1, source_target_pairs={{0,1},{1,0},{2,3},{3,2},{4,5},{5,4},{6,7},{7,6},{8,9},{9,8},{10,11... | collective-permute-start | bytes 638984 | tf_op jit(solution)/shard_map/ppermute | solution.py:872
  40.9 10.0 %collective-permute-start.10 = (bf16[2,16,3328]{2,1,0:T(8,128)(2,1)S(1)}, bf16[2,16,3328]{2,1,0:T(8,128)(2,1)S(1)}, u32[]{:S(2)}, u32[]{:S(2)}) collective-permute-start(bf16[2,16,3328]{2,1,0:T(8,128)(2,1)S(1)} %collective-permute-done.8.refs_9_), channel_id=1, source_target_pairs={{0,1},{1,0},{2,3},{3,2},{4,5},{5,4},{6,7},{7,6},{8,9},{9,8},{10,11... | collective-permute-start | bytes 638984 | tf_op jit(solution)/shard_map/ppermute | solution.py:872
  52.0 31.1 %all-to-all-start = ((bf16[8,256,512]{2,1,0:T(8,128)(2,1)}), bf16[8,256,512]{2,1,0:T(8,128)(2,1)}, u32[]{:S(2)}, u32[]{:S(2)}) async-start(bf16[8,256,512]{2,1,0:T(8,128)(2,1)} %shard_map.214), calls=%async_computation | async-start | bytes 4194304 | tf_op jit(solution)/shard_map/all_to_all | solution.py:946
  83.1 31.0 %all-to-all-start.1 = ((bf16[8,256,512]{2,1,0:T(8,128)(2,1)}), bf16[8,256,512]{2,1,0:T(8,128)(2,1)}, u32[]{:S(2)}, u32[]{:S(2)}) async-start(bf16[8,256,512]{2,1,0:T(8,128)(2,1)} %get-tuple-element.92), calls=%async_computation.1 | async-start | bytes 4194304 | tf_op jit(solution)/shard_map/all_to_all | solution.py:946
  114.1 31.5 %all-to-all-start.2 = ((bf16[8,256,512]{2,1,0:T(8,128)(2,1)}), bf16[8,256,512]{2,1,0:T(8,128)(2,1)}, u32[]{:S(2)}, u32[]{:S(2)}) async-start(bf16[8,256,512]{2,1,0:T(8,128)(2,1)} %shard_map.215), calls=%async_computation.2 | async-start | bytes 4194304 | tf_op jit(solution)/shard_map/all_to_all | solution.py:946
  172.0 31.0 %all-to-all-start.3 = ((bf16[8,256,512]{2,1,0:T(8,128)(2,1)}), bf16[8,256,512]{2,1,0:T(8,128)(2,1)}, u32[]{:S(2)}, u32[]{:S(2)}) async-start(bf16[8,256,512]{2,1,0:T(8,128)(2,1)} %bitcast.41), calls=%async_computation.3 | async-start | bytes 4194304 | tf_op jit(solution)/shard_map/all_to_all | solution.py:946
  203.0 31.0 %all-to-all-start.4 = ((bf16[8,256,512]{2,1,0:T(8,128)(2,1)}), bf16[8,256,512]{2,1,0:T(8,128)(2,1)}, u32[]{:S(2)}, u32[]{:S(2)}) async-start(bf16[8,256,512]{2,1,0:T(8,128)(2,1)} %bitcast.40), calls=%async_computation.4 | async-start | bytes 4194304 | tf_op jit(solution)/shard_map/all_to_all | solution.py:946
  234.0 33.5 %all-to-all-start.5 = ((bf16[8,128,512]{2,1,0:T(8,128)(2,1)}), bf16[8,128,512]{2,1,0:T(8,128)(2,1)}, u32[]{:S(2)}, u32[]{:S(2)}) async-start(bf16[8,128,512]{2,1,0:T(8,128)(2,1)} %get-tuple-element.112), calls=%async_computation.5 | async-start | bytes 2097152 | tf_op jit(solution)/shard_map/all_to_all | solution.py:946
  276.7 20.2 %all-to-all-start.8 = ((bf16[8,128,512]{2,1,0:T(8,128)(2,1)}), bf16[8,128,512]{2,1,0:T(8,128)(2,1)}, u32[]{:S(2)}, u32[]{:S(2)}) async-start(bf16[8,128,512]{2,1,0:T(8,128)(2,1)} %get-tuple-element.119), calls=%async_computation.8 | async-start | bytes 2097152 | tf_op jit(solution)/shard_map/all_to_all | solution.py:946
  296.9 47.4 %all-to-all-start.7 = ((bf16[8,256,512]{2,1,0:T(8,128)(2,1)}), bf16[8,256,512]{2,1,0:T(8,128)(2,1)}, u32[]{:S(2)}, u32[]{:S(2)}) async-start(bf16[8,256,512]{2,1,0:T(8,128)(2,1)} %bitcast.38), calls=%async_computation.7 | async-start | bytes 4194304 | tf_op jit(solution)/shard_map/all_to_all | solution.py:946
  301.3 179.7 %reduce-scatter.2.cloned.1.call-start = ((), (), s32[]{:S(2)}) async-start(), calls=%async_computation.14 | async-start | bytes 5242880 | tf_op jit(solution)/shard_map/reduce_scatter | solution.py:1133
  420.6 24.7 %all-to-all-start.11 = ((bf16[8,4,16,1536]{3,2,1,0:T(8,128)(2,1)}), bf16[8,4,16,1536]{3,2,1,0:T(8,128)(2,1)S(1)}, u32[]{:S(2)}, u32[]{:S(2)}) async-start(bf16[8,4,16,1536]{3,2,1,0:T(8,128)(2,1)} %get-tuple-element.139), calls=%async_computation.11 | async-start | bytes 3145728 | tf_op jit(solution)/shard_map/all_to_all | solution.py:946
  445.2 15.0 %all-to-all-start.10 = ((bf16[4,4,16,1792]{3,2,1,0:T(8,128)(2,1)}), bf16[4,4,16,1792]{3,2,1,0:T(8,128)(2,1)S(1)}, u32[]{:S(2)}, u32[]{:S(2)}) async-start(bf16[4,4,16,1792]{3,2,1,0:T(8,128)(2,1)} %fusion), calls=%async_computation.10 | async-start | bytes 1835008 | tf_op jit(solution)/shard_map/all_to_all | solution.py:1214
  461.2 17.1 %all-to-all-start.12 = ((bf16[4,16,3328]{2,1,0:T(8,128)(2,1)}), bf16[4,16,3328]{2,1,0:T(8,128)(2,1)S(1)}, u32[]{:S(2)}, u32[]{:S(2)}) async-start(bf16[4,16,3328]{2,1,0:T(8,128)(2,1)} %pad_maximum_fusion.2), calls=%async_computation.12 | async-start | bytes 851968 | tf_op jit(solution)/shard_map/all_to_all | solution.py:1248
  (20 other events, 219.8 us)
Sparse Core Ops, SparseCore 0:
  28.0 80.2 all-gather.2
  344.4 79.8 reduce-scatter.1
